TPU v7x, 32 devices: a whole 2x2x4 slice. The times are simulated.
32 devices in a mesh: dev: 32 (over z, y, x, core).
Axes of the slice: x: 2, y: 2, z: 4, core: 2. Of those that a mesh axis runs over, the one named last changes fastest.
Arguments:
- tokens_in: float32 [32768, 1024], P('dev'), may hold values from -6 to 6
- attn_gain: float32 [1024], P('dev'), may hold values from 0.25 to 1.75
- attn_bias: float32 [1024], P('dev'), may hold values from -3 to 3
- query_mat: float32 [1024, 1024], P('dev'), may hold values from -0.1875 to 0.1875
- query_bias: float32 [1024], P('dev'), may hold values from -3 to 3
- key_mat: float32 [1024, 1024], P('dev'), may hold values from -0.1875 to 0.1875
- value_mat: float32 [1024, 1024], P('dev'), may hold values from -0.1875 to 0.1875
- value_bias: float32 [1024], P('dev'), may hold values from -3 to 3
- output_mat: float32 [1024, 1024], P('dev'), may hold values from -4 to 4
- output_bias: float32 [1024], P('dev'), may hold values from -3 to 3
- mlp_gain: float32 [1024], P('dev'), may hold values from 0.25 to 1.75
- mlp_bias: float32 [1024], P('dev'), may hold values from -3 to 3
- expand_mat: float32 [1024, 4096], P('dev'), may hold values from -0.1875 to 0.1875
- expand_bias: float32 [4096], P('dev'), may hold values from -3 to 3
- reduce_mat: float32 [4096, 1024], P('dev'), may hold values from -0.09375 to 0.09375
- reduce_bias: float32 [1024], P('dev'), may hold values from -3 to 3
- image_ids: int32 [32768], P('dev'), may hold values from 0 to 74, never falling along the last dimension, each value on 1 to 577 neighbouring positions
- clip_flags: int32 [16], replicated, may hold values 0 or 1
- out_grad: float32 [32768, 1024], P('dev'), may hold values from -6 to 6
Outputs:
- block_out: float32 [32768, 1024], P('dev')
- tokens_grad: float32 [32768, 1024], P('dev')
- query_clipped: float32 [1024, 1024], P('dev')
- key_clipped: float32 [1024, 1024], P('dev')
- attn_gain_grad: float32 [1024], P('dev')
- attn_bias_grad: float32 [1024], P('dev')
- query_mat_grad: float32 [1024, 1024], P('dev')
- query_bias_grad: float32 [1024], P('dev')
- key_mat_grad: float32 [1024, 1024], P('dev')
- value_mat_grad: float32 [1024, 1024], P('dev')
- value_bias_grad: float32 [1024], P('dev')
- output_mat_grad: float32 [1024, 1024], P('dev')
- output_bias_grad: float32 [1024], P('dev')
- mlp_gain_grad: float32 [1024], P('dev')
- mlp_bias_grad: float32 [1024], P('dev')
- expand_mat_grad: float32 [1024, 4096], P('dev')
- expand_bias_grad: float32 [4096], P('dev')
- reduce_mat_grad: float32 [4096, 1024], P('dev')
- reduce_bias_grad: float32 [1024], P('dev')
Inputs may be any that keep to these rules, and one draw needn't show every extreme that they name: `image_ids`: image numbers never fall along the tokens; every number occurs; each image has 1 to 577 tokens, and some image has exactly 577.
All inputs are finite; a program needn't handle non-finite values.
Results may differ from a plain program's by a relative error of at most 0.012.
The roundings to bfloat16 on the way count: a program that leaves them out, or rounds other values in their place, can miss the bound.
Values may be sent and summed in bfloat16 or wider, within the bound.
No kernel may reach another device: no remote copies, remote signals or barrier semaphores. Data moves between devices by JAX's collectives and lax.ppermute only.
A program may use at most 448 MiB of HBM per device.

v0:
```python
import jax
import jax.numpy as jnp
from jax import lax
from jax.sharding import PartitionSpec as P

H = 16
HD = 64
LEN = 577
QB = 512


NORM_EPS = 1e-05
CLIP_TAU = 3.0
GELU_COEF = 1.702
NEG_FILL = -1e30


def extended(value, sides, width):
    for axis, dim in sides:
        peers, length = (lax.axis_size(axis), value.shape[dim])
        up = [(i, (i + 1) % peers) for i in range(peers - 1)]
        down = [(j, i) for i, j in up]
        last = lax.slice_in_dim(value, length - width, length, axis=dim)
        leading = lax.slice_in_dim(value, 0, width, axis=dim)
        before = lax.ppermute(last, axis, up)
        after = lax.ppermute(leading, axis, down)
        value = jnp.concatenate([before, value, after], axis=dim)
    return value


def plain_dot(lhs_mat, rhs_mat):
    return jnp.dot(lhs_mat, rhs_mat, preferred_element_type=jnp.float32)


def rows_dot(lhs_mat, rhs_mat):
    return lax.dot_general(
        lhs_mat, rhs_mat, (((0,), (0,)), ((), ())), preferred_element_type=jnp.float32
    )


def back_dot(lhs_mat, rhs_mat):
    return lax.dot_general(
        lhs_mat, rhs_mat, (((1,), (1,)), ((), ())), preferred_element_type=jnp.float32
    )


def norm_stats(values):
    centre = values - jnp.mean(values, axis=1, keepdims=True)
    inv_std = lax.rsqrt(jnp.mean(centre * centre, axis=1, keepdims=True) + NORM_EPS)
    return (centre * inv_std, inv_std)


def norm_back(grad_out, gain, normal, inv_std):
    scaled = grad_out * gain
    return inv_std * (
        scaled
        - jnp.mean(scaled, axis=1, keepdims=True)
        - normal * jnp.mean(scaled * normal, axis=1, keepdims=True)
    )


def column_sums(values):
    return jnp.sum(values.astype(jnp.float32), axis=0)


def local(
    tokens_in,
    attn_gain,
    attn_bias,
    query_mat,
    query_bias,
    key_mat,
    value_mat,
    value_bias,
    output_mat,
    output_bias,
    mlp_gain,
    mlp_bias,
    expand_mat,
    expand_bias,
    reduce_mat,
    reduce_bias,
    image_ids,
    clip_flags,
    out_grad,
):
    bf16 = jnp.bfloat16
    f32 = jnp.float32
    low_query = query_mat.astype(bf16)
    low_key = key_mat.astype(bf16)
    low_value = value_mat.astype(bf16)
    low_output = output_mat.astype(bf16)
    low_expand = expand_mat.astype(bf16)
    low_reduce = reduce_mat.astype(bf16)
    low_again = attn_gain.astype(bf16)
    low_abias = attn_bias.astype(bf16)
    low_qbias = query_bias.astype(bf16)
    low_vbias = value_bias.astype(bf16)
    low_obias = output_bias.astype(bf16)
    low_mgain = mlp_gain.astype(bf16)
    low_mbias = mlp_bias.astype(bf16)
    low_ebias = expand_bias.astype(bf16)
    low_rbias = reduce_bias.astype(bf16)
    gathered = (
        lax.all_gather(low_query, "dev", axis=0, tiled=True),
        lax.all_gather(low_key, "dev", axis=0, tiled=True),
        lax.all_gather(low_value, "dev", axis=0, tiled=True),
        lax.all_gather(low_output, "dev", axis=0, tiled=True),
        lax.all_gather(low_expand, "dev", axis=0, tiled=True),
        lax.all_gather(low_reduce, "dev", axis=0, tiled=True),
        lax.all_gather(low_again, "dev", axis=0, tiled=True),
        lax.all_gather(low_abias, "dev", axis=0, tiled=True),
        lax.all_gather(low_qbias, "dev", axis=0, tiled=True),
        lax.all_gather(low_vbias, "dev", axis=0, tiled=True),
        lax.all_gather(low_obias, "dev", axis=0, tiled=True),
        lax.all_gather(low_mgain, "dev", axis=0, tiled=True),
        lax.all_gather(low_mbias, "dev", axis=0, tiled=True),
        lax.all_gather(low_ebias, "dev", axis=0, tiled=True),
        lax.all_gather(low_rbias, "dev", axis=0, tiled=True),
    )
    w_query, w_key, w_value, w_output, w_expand, w_reduce = gathered[:6]
    (
        gain_one,
        bias_one,
        bias_query,
        bias_value,
        bias_output,
        gain_two,
        bias_two,
        bias_expand,
        bias_reduce,
    ) = [vector.astype(f32) for vector in gathered[6:]]
    local_rows = tokens_in.shape[0]
    blocks = local_rows // QB
    rim_rows = LEN - 1
    key_window = QB + 2 * rim_rows
    score_scale = HD ** (-0.5)
    normal_one, inv_one = norm_stats(tokens_in)
    normed = (normal_one * gain_one + bias_one).astype(bf16)
    queries = (plain_dot(normed, w_query) + bias_query).astype(bf16)
    keys = plain_dot(normed, w_key).astype(bf16)
    values = (plain_dot(normed, w_value) + bias_value).astype(bf16)
    stacked = jnp.stack([keys, values])
    near_kv = extended(stacked, (("dev", 1),), rim_rows)
    own_ids = image_ids + 1
    near_ids = extended(own_ids, (("dev", 0),), rim_rows)

    def block_inputs(block_no):
        start = block_no * QB
        query_rows = lax.dynamic_slice_in_dim(queries, start, QB, 0).reshape(QB, H, HD)
        near_rows = lax.dynamic_slice_in_dim(near_kv, start, key_window, 1)
        key_rows = near_rows[0].reshape(key_window, H, HD)
        value_rows = near_rows[1].reshape(key_window, H, HD)
        query_ids = lax.dynamic_slice_in_dim(own_ids, start, QB, 0)
        window_ids = lax.dynamic_slice_in_dim(near_ids, start, key_window, 0)
        allowed = (query_ids[:, None] == window_ids[None, :])[None]
        scores = (
            jnp.einsum("qhd,khd->hqk", query_rows, key_rows, preferred_element_type=f32)
            * score_scale
        )
        return (query_rows, key_rows, value_rows, allowed, scores)

    def attend(block_no):
        query_rows, key_rows, value_rows, allowed, scores = block_inputs(block_no)
        masked = jnp.where(allowed, scores, NEG_FILL)
        row_top = jnp.max(masked, axis=2, keepdims=True)
        weights = jnp.where(allowed, jnp.exp(masked - row_top), 0.0)
        row_total = jnp.sum(weights, axis=2, keepdims=True)
        prob_rows = (weights / row_total).astype(bf16)
        attn_mixed = jnp.einsum("hqk,khd->qhd", prob_rows, value_rows, preferred_element_type=f32)
        return (
            attn_mixed.reshape(QB, -1),
            (row_top + jnp.log(row_total))[:, :, 0],
            jnp.max(row_top[:, :, 0], axis=1),
        )

    attn_mixed, log_sums, block_top = lax.map(attend, jnp.arange(blocks, dtype=jnp.int32))
    mixed_low = attn_mixed.reshape(local_rows, -1).astype(bf16)
    global_top = lax.pmax(jnp.max(block_top, axis=0), "dev")
    middle = tokens_in + plain_dot(mixed_low, w_output) + bias_output
    normal_two, inv_two = norm_stats(middle)
    normed_two = (normal_two * gain_two + bias_two).astype(bf16)
    hidden = plain_dot(normed_two, w_expand) + bias_expand
    sigma = jax.nn.sigmoid(GELU_COEF * hidden)
    active = (hidden * sigma).astype(bf16)
    block_out = middle + plain_dot(active, w_reduce) + bias_reduce
    regathered = (
        lax.all_gather(low_query, "dev", axis=0, tiled=True),
        lax.all_gather(low_key, "dev", axis=0, tiled=True),
        lax.all_gather(low_value, "dev", axis=0, tiled=True),
        lax.all_gather(low_output, "dev", axis=0, tiled=True),
        lax.all_gather(low_expand, "dev", axis=0, tiled=True),
        lax.all_gather(low_reduce, "dev", axis=0, tiled=True),
        lax.all_gather(low_again, "dev", axis=0, tiled=True),
        lax.all_gather(low_mgain, "dev", axis=0, tiled=True),
    )
    w_query, w_key, w_value, w_output, w_expand, w_reduce = regathered[:6]
    gain_one = regathered[6].astype(f32)
    gain_two = regathered[7].astype(f32)
    branch_grad = out_grad.astype(bf16)
    reduce_bias_grad = column_sums(branch_grad)
    reduce_mat_grad = rows_dot(active, branch_grad)
    hidden_grad = (
        back_dot(branch_grad, w_reduce) * (sigma + GELU_COEF * hidden * sigma * (1.0 - sigma))
    ).astype(bf16)
    expand_bias_grad = column_sums(hidden_grad)
    expand_mat_grad = rows_dot(normed_two, hidden_grad)
    normed_two_grad = back_dot(hidden_grad, w_expand)
    mlp_gain_grad = jnp.sum(normed_two_grad * normal_two, axis=0)
    mlp_bias_grad = jnp.sum(normed_two_grad, axis=0)
    middle_grad = out_grad + norm_back(normed_two_grad, gain_two, normal_two, inv_two)
    attn_grad = middle_grad.astype(bf16)
    output_bias_grad = column_sums(attn_grad)
    output_mat_grad = rows_dot(mixed_low, attn_grad)
    mixed_grad = back_dot(attn_grad, w_output).astype(bf16)

    def attend_back(kv_accum, block_no):
        query_rows, key_rows, value_rows, allowed, scores = block_inputs(block_no)
        grad_rows = lax.dynamic_slice_in_dim(mixed_grad, block_no * QB, QB, 0).reshape(QB, H, HD)
        prob_rows = jnp.where(allowed, jnp.exp(scores - log_sums[block_no][:, :, None]), 0.0)
        prob_grad = jnp.einsum("qhd,khd->hqk", grad_rows, value_rows, preferred_element_type=f32)
        row_inner = jnp.sum(prob_rows * prob_grad, axis=2, keepdims=True)
        score_grad = (prob_rows * (prob_grad - row_inner)).astype(bf16)
        query_part = (
            jnp.einsum("hqk,khd->qhd", score_grad, key_rows, preferred_element_type=f32)
            * score_scale
        )
        key_part = (
            jnp.einsum("hqk,qhd->khd", score_grad, query_rows, preferred_element_type=f32)
            * score_scale
        )
        value_part = jnp.einsum(
            "hqk,qhd->khd", prob_rows.astype(bf16), grad_rows, preferred_element_type=f32
        )
        update = jnp.stack([key_part.reshape(key_window, -1), value_part.reshape(key_window, -1)])
        current = lax.dynamic_slice_in_dim(kv_accum, block_no * QB, key_window, 1)
        kv_accum = lax.dynamic_update_slice_in_dim(kv_accum, current + update, block_no * QB, 1)
        return (kv_accum, query_part.reshape(QB, -1))

    kv_start = jnp.zeros((2, local_rows + 2 * rim_rows, queries.shape[1]), f32)
    kv_grad, query_parts = lax.scan(attend_back, kv_start, jnp.arange(blocks, dtype=jnp.int32))
    outgoing = jnp.concatenate([kv_grad[:, :rim_rows], kv_grad[:, -rim_rows:]], axis=1)
    incoming = extended(outgoing.astype(jnp.bfloat16), (("dev", 1),), rim_rows).astype(
        outgoing.dtype
    )
    own_grad = kv_grad[:, rim_rows : rim_rows + local_rows]
    own_grad = own_grad.at[:, :rim_rows].add(incoming[:, :rim_rows])
    own_grad = own_grad.at[:, local_rows - rim_rows :].add(incoming[:, -rim_rows:])
    query_grad = query_parts.reshape(local_rows, -1).astype(bf16)
    key_grad = own_grad[0].astype(bf16)
    value_grad = own_grad[1].astype(bf16)
    query_mat_grad = rows_dot(normed, query_grad)
    query_bias_grad = column_sums(query_grad)
    key_mat_grad = rows_dot(normed, key_grad)
    value_mat_grad = rows_dot(normed, value_grad)
    value_bias_grad = column_sums(value_grad)
    normed_grad = (
        back_dot(query_grad, w_query) + back_dot(key_grad, w_key) + back_dot(value_grad, w_value)
    )
    attn_gain_grad = jnp.sum(normed_grad * normal_one, axis=0)
    attn_bias_grad = jnp.sum(normed_grad, axis=0)
    tokens_grad = middle_grad + norm_back(normed_grad, gain_one, normal_one, inv_one)
    summed = (
        lax.psum_scatter(query_mat_grad, "dev", scatter_dimension=0, tiled=True),
        lax.psum_scatter(key_mat_grad, "dev", scatter_dimension=0, tiled=True),
        lax.psum_scatter(value_mat_grad, "dev", scatter_dimension=0, tiled=True),
        lax.psum_scatter(output_mat_grad, "dev", scatter_dimension=0, tiled=True),
        lax.psum_scatter(expand_mat_grad, "dev", scatter_dimension=0, tiled=True),
        lax.psum_scatter(reduce_mat_grad, "dev", scatter_dimension=0, tiled=True),
        lax.psum_scatter(attn_gain_grad, "dev", scatter_dimension=0, tiled=True),
        lax.psum_scatter(attn_bias_grad, "dev", scatter_dimension=0, tiled=True),
        lax.psum_scatter(query_bias_grad, "dev", scatter_dimension=0, tiled=True),
        lax.psum_scatter(value_bias_grad, "dev", scatter_dimension=0, tiled=True),
        lax.psum_scatter(output_bias_grad, "dev", scatter_dimension=0, tiled=True),
        lax.psum_scatter(mlp_gain_grad, "dev", scatter_dimension=0, tiled=True),
        lax.psum_scatter(mlp_bias_grad, "dev", scatter_dimension=0, tiled=True),
        lax.psum_scatter(expand_bias_grad, "dev", scatter_dimension=0, tiled=True),
        lax.psum_scatter(reduce_bias_grad, "dev", scatter_dimension=0, tiled=True),
    )
    ratio = CLIP_TAU / jnp.maximum(global_top, CLIP_TAU)
    factor = jnp.where(clip_flags == 1, jnp.sqrt(ratio), 1.0)
    columns = jnp.repeat(factor, HD)
    query_clipped = query_mat * columns[None, :]
    key_clipped = key_mat * columns[None, :]
    return (
        block_out,
        tokens_grad,
        query_clipped,
        key_clipped,
        summed[6],
        summed[7],
        summed[0],
        summed[8],
        summed[1],
        summed[2],
        summed[9],
        summed[3],
        summed[10],
        summed[11],
        summed[12],
        summed[4],
        summed[13],
        summed[5],
        summed[14],
    )


def solution(mesh):
    return jax.shard_map(
        local,
        mesh=mesh,
        in_specs=(
            P("dev", None),
            P("dev"),
            P("dev"),
            P("dev", None),
            P("dev"),
            P("dev", None),
            P("dev", None),
            P("dev"),
            P("dev", None),
            P("dev"),
            P("dev"),
            P("dev"),
            P("dev", None),
            P("dev"),
            P("dev", None),
            P("dev"),
            P("dev"),
            P(),
            P("dev", None),
        ),
        out_specs=(
            P("dev", None),
            P("dev", None),
            P("dev", None),
            P("dev", None),
            P("dev"),
            P("dev"),
            P("dev", None),
            P("dev"),
            P("dev", None),
            P("dev", None),
            P("dev"),
            P("dev", None),
            P("dev"),
            P("dev"),
            P("dev"),
            P("dev", None),
            P("dev"),
            P("dev", None),
            P("dev"),
        ),
        check_vma=False,
    )
```

profile of v0, /device:TPU:0, one launch (start us, length us, event | category | flops | bytes accessed | tf_op | source)
XLA Modules:
  0.0 1832.4 jit_solution(3349560916668019602)
XLA Ops:
  30.3 42.5 %all-reduce.18 = (bf16[1024]{0:T(1024)(128)(2,1)S(1)}, bf16[1024]{0:T(1024)(128)(2,1)S(1)}, bf16[1024]{0:T(1024)(128)(2,1)S(1)}, bf16[1024]{0:T(1024)(128)(2,1)S...) all-reduce(bf16[1024]{0:T(1024)(128)(2,1)S(1)} %dynamic-update-slic, ...), channel_id=1, replica_groups=mesh['dev'=32] {'dev'}, use_global_device_ids=true, to_apply=%add.4 | all-reduce | flops 8192 | bytes 32768
  82.9 46.6 %all-gather.10.cloned.1.call-done = bf16[1024,1024]{1,0:T(8,128)(2,1)} async-done(((bf16[32,1024]{1,0:T(8,128)(2,1)}), bf16[1024,1024]{1,0:T(8,128)(2,1)}) %all-gather.10.cloned.1.call-update) | async-done | bytes 2097168 | tf_op jit(solution)/shard_map/all_gather | solution.py:107
  149.6 80.5 %all-gather = bf16[32,1,128]{2,1,0:T(2,128)(2,1)S(1)} all-gather(bf16[1,1,128]{2,1,0:T(2,128)(2,1)S(1)} %convert_bitcast_fusion.1), channel_id=1, replica_groups=mesh['dev'=32] {'dev'}, dimensions={0}, use_global_device_ids=true | all-gather | bytes 8448 | tf_op jit(solution)/shard_map/all_gather | solution.py:118
  265.8 158.1 %while.28 = (s32[]{:T(128)}, bf16[2,512,1024]{2,1,0:T(8,128)(2,1)}, f32[2,16,512]{2,1,0:T(8,128)S(1)}, f32[2,16]{1,0:T(2,128)S(1)}, s32[2]{0:T(128)S(1)}, /*inde...) while((s32[]{:T(128)}, bf16[2,512,1024]{2,1,0:T(8,128)(2,1)}, ...), condition=%wide.region_6.7_spmd, body=%wide.region_2.6_spmd.sunk | while | flops 3694977024 | bytes 196110288 | solution.py:177
  273.2 19.9 %fusion.92 = (f32[16,512]{1,0:T(8,128)S(1)}, f32[16,512,1664]{2,1,0:T(8,128)}) fusion(pred[512,1664]{1,0:T(8,128)(4,1)S(1)} %broadcast_compare_fusion.4, bf16[512,16,64]{0,2,1:T(8,128)(2,1)S(1)} %bitcast.149, bf16[1664,16,64]{0,2,1:T(8,128)(2,1)S(1)} %bitcast.144), kind=kOutput, calls=%fused_computation.5.clone.1 | convolution fusion | flops 1785716736 | bytes 59867136 | tf_op jit(solution)/shard_map/while/body/eval_jaxpr/qhd,khd->hqk/dot_general | solution.py:158
  293.1 24.4 %fusion.93 = (f32[16]{0:T(128)S(1)}, f32[16,512]{1,0:T(8,128)S(1)}) fusion(f32[16,512,1664]{2,1,0:T(8,128)} %get-tuple-element.473, pred[512,1664]{1,0:T(8,128)(4,1)S(1)} %broadcast_compare_fusion.4, f32[16,512]{1,0:T(8,128)S(1)} %get-tuple-element.474), kind=kLoop, calls=%fused_computation.4.clone.1 | loop fusion | flops 81780720 | bytes 55443520 | tf_op jit(solution)/shard_map/while/body/eval_jaxpr/reduce_max | solution.py:174
  317.5 24.5 %fusion.94 = bf16[16,64,512]{2,1,0:T(8,128)(2,1)} fusion(bf16[1664,16,64]{0,2,1:T(8,128)(2,1)} %bitcast.153, f32[16,512,1664]{2,1,0:T(8,128)} %get-tuple-element.473, f32[16,512]{1,0:T(8,128)S(1)} %get-tuple-element.475, f32[16,512]{1,0:T(8,128)S(1)} %get-tuple-element.474, pred[512,1664]{1,0:T(8,128)(4,1)S(1)} %broadcast_compare_fusion.4), kind=kOutput, calls=%fused_computation.6.clone.1 | convolution fusion | flops 1826619392 | bytes 59899904 | tf_op jit(solution)/shard_map/while/body/eval_jaxpr/hqk,khd->qhd/dot_general | solution.py:170
  371.9 24.4 %fusion.93 = (f32[16]{0:T(128)S(1)}, f32[16,512]{1,0:T(8,128)S(1)}) fusion(f32[16,512,1664]{2,1,0:T(8,128)} %get-tuple-element.473, pred[512,1664]{1,0:T(8,128)(4,1)S(1)} %broadcast_compare_fusion.4, f32[16,512]{1,0:T(8,128)S(1)} %get-tuple-element.474), kind=kLoop, calls=%fused_computation.4.clone.1 | loop fusion | flops 81780720 | bytes 55443520 | tf_op jit(solution)/shard_map/while/body/eval_jaxpr/reduce_max | solution.py:174
  396.4 24.5 %fusion.94 = bf16[16,64,512]{2,1,0:T(8,128)(2,1)} fusion(bf16[1664,16,64]{0,2,1:T(8,128)(2,1)} %bitcast.153, f32[16,512,1664]{2,1,0:T(8,128)} %get-tuple-element.473, f32[16,512]{1,0:T(8,128)S(1)} %get-tuple-element.475, f32[16,512]{1,0:T(8,128)S(1)} %get-tuple-element.474, pred[512,1664]{1,0:T(8,128)(4,1)S(1)} %broadcast_compare_fusion.4), kind=kOutput, calls=%fused_computation.6.clone.1 | convolution fusion | flops 1826619392 | bytes 59899904 | tf_op jit(solution)/shard_map/while/body/eval_jaxpr/hqk,khd->qhd/dot_general | solution.py:170
  449.6 22.2 %convert_reduce_fusion = (f32[4096]{0:T(1024)}, bf16[1024,4096]{1,0:T(8,128)(2,1)}) fusion(f32[1024,4096]{1,0:T(8,128)} %fusion.27, f32[4096]{0:T(1024)S(1)} %bitcast.160, bf16[4096,1024]{1,0:T(8,128)(2,1)} %all-gather.18.cloned.1.call-done, f32[1024,1024]{1,0:T(8,128)} %param.45), kind=kOutput, calls=%fused_computation.36 | convolution fusion | flops 8645505024 | bytes 37781504 | tf_op jit(solution)/shard_map/dot_general | solution.py:42
  526.4 484.2 %while.29 = (s32[]{:T(128)}, f32[2,2176,1024]{2,1,0:T(8,128)}, bf16[2,512,1024]{2,1,0:T(8,128)(2,1)}, s32[2]{0:T(128)S(1)}, bf16[1024,1024]{0,1:T(8,128)(2,1)S(1...) while((s32[]{:T(128)}, f32[2,2176,1024]{2,1,0:T(8,128)}, ...), condition=%wide.region_13.14_spmd, body=%wide.region_11.13_spmd.sunk | while | flops 8939036672 | bytes 658601856 | solution.py:241
  567.1 22.2 %fusion.105 = f32[16,512,1664]{2,1,0:T(8,128)} fusion(bf16[512,16,64]{0,2,1:T(8,128)(2,1)} %bitcast.146, bf16[1664,16,64]{0,2,1:T(8,128)(2,1)S(1)} %bitcast.139), kind=kOutput, calls=%fused_computation.108.clone.1 | convolution fusion | flops 1744830464 | bytes 58982400 | tf_op jit(solution)/shard_map/while/body/eval_jaxpr/qhd,khd->hqk/dot_general | solution.py:158
  589.3 27.6 %fusion.106 = f32[16,64,1664]{2,1,0:T(8,128)} fusion(bf16[512,16,64]{0,2,1:T(8,128)(2,1)} %bitcast.150, f32[16,512,1664]{2,1,0:T(8,128)} %fusion.105, f32[16,512]{1,0:T(8,128)S(1)} %dynamic-slice_bitcast_fusion.2, pred[512,1664]{1,0:T(8,128)(4,1)} %broadcast_compare_fusion.5), kind=kOutput, calls=%fused_computation.20.clone.1 | convolution fusion | flops 1799356416 | bytes 63275008 | tf_op jit(solution)/shard_map/while/body/eval_jaxpr/hqk,qhd->khd/dot_general | solution.py:232
  616.9 40.2 %multiply_reduce_fusion.10 = (f32[16,512]{1,0:T(8,128)S(1)}, f32[16,512,1664]{2,1,0:T(8,128)}) fusion(f32[16,512,1664]{2,1,0:T(8,128)} %fusion.105, f32[16,512]{1,0:T(8,128)S(1)} %dynamic-slice_bitcast_fusion.2, pred[512,1664]{1,0:T(8,128)(4,1)S(1)} %copy-done, bf16[512,16,64]{0,2,1:T(8,128)(2,1)S(1)} %bitcast.151, ...), kind=kOutput, calls=%fused_computation.17.clone.1 | convolution fusion | flops 1812979712 | bytes 114425856 | tf_op jit(solution)/shard_map/while/body/eval_jaxpr/qhd,khd->hqk/dot_general | solution.py:221
  657.1 43.8 %multiply_convert_fusion.6 = bf16[16,512,1664]{2,1,0:T(8,128)(2,1)} fusion(f32[16,512,1664]{2,1,0:T(8,128)} %get-tuple-element.489, f32[16,512,1664]{2,1,0:T(8,128)} %fusion.105, f32[16,512]{1,0:T(8,128)S(1)} %get-tuple-element.490, f32[16,512]{1,0:T(8,128)S(1)} %dynamic-slice_bitcast_fusion.2, pred[512,1664]{1,0:T(8,128)(4,1)} %broadcast_compare_fusion.5), kind=kLoop, calls=%fused_computation.16.clone.1 | loop fusion | flops 81788928 | bytes 137232384 | tf_op jit(solution)/shard_map/while/body/eval_jaxpr/convert_element_type | solution.py:223
  809.1 22.0 %fusion.105 = f32[16,512,1664]{2,1,0:T(8,128)} fusion(bf16[512,16,64]{0,2,1:T(8,128)(2,1)} %bitcast.146, bf16[1664,16,64]{0,2,1:T(8,128)(2,1)S(1)} %bitcast.139), kind=kOutput, calls=%fused_computation.108.clone.1 | convolution fusion | flops 1744830464 | bytes 58982400 | tf_op jit(solution)/shard_map/while/body/eval_jaxpr/qhd,khd->hqk/dot_general | solution.py:158
  831.0 27.5 %fusion.106 = f32[16,64,1664]{2,1,0:T(8,128)} fusion(bf16[512,16,64]{0,2,1:T(8,128)(2,1)} %bitcast.150, f32[16,512,1664]{2,1,0:T(8,128)} %fusion.105, f32[16,512]{1,0:T(8,128)S(1)} %dynamic-slice_bitcast_fusion.2, pred[512,1664]{1,0:T(8,128)(4,1)} %broadcast_compare_fusion.5), kind=kOutput, calls=%fused_computation.20.clone.1 | convolution fusion | flops 1799356416 | bytes 63275008 | tf_op jit(solution)/shard_map/while/body/eval_jaxpr/hqk,qhd->khd/dot_general | solution.py:232
  858.5 40.1 %multiply_reduce_fusion.10 = (f32[16,512]{1,0:T(8,128)S(1)}, f32[16,512,1664]{2,1,0:T(8,128)}) fusion(f32[16,512,1664]{2,1,0:T(8,128)} %fusion.105, f32[16,512]{1,0:T(8,128)S(1)} %dynamic-slice_bitcast_fusion.2, pred[512,1664]{1,0:T(8,128)(4,1)S(1)} %copy-done, bf16[512,16,64]{0,2,1:T(8,128)(2,1)S(1)} %bitcast.151, ...), kind=kOutput, calls=%fused_computation.17.clone.1 | convolution fusion | flops 1812979712 | bytes 114425856 | tf_op jit(solution)/shard_map/while/body/eval_jaxpr/qhd,khd->hqk/dot_general | solution.py:221
  898.6 43.8 %multiply_convert_fusion.6 = bf16[16,512,1664]{2,1,0:T(8,128)(2,1)} fusion(f32[16,512,1664]{2,1,0:T(8,128)} %get-tuple-element.489, f32[16,512,1664]{2,1,0:T(8,128)} %fusion.105, f32[16,512]{1,0:T(8,128)S(1)} %get-tuple-element.490, f32[16,512]{1,0:T(8,128)S(1)} %dynamic-slice_bitcast_fusion.2, pred[512,1664]{1,0:T(8,128)(4,1)} %broadcast_compare_fusion.5), kind=kLoop, calls=%fused_computation.16.clone.1 | loop fusion | flops 81788928 | bytes 137232384 | tf_op jit(solution)/shard_map/while/body/eval_jaxpr/convert_element_type | solution.py:223
  1101.2 98.5 %pmax.7 = f32[16]{0:T(128)S(1)} all-reduce(f32[16]{0:T(128)S(1)} %reduce_max.27), channel_id=1, replica_groups=mesh['dev'=32] {'dev'}, use_global_device_ids=true, to_apply=%region_17.18 | all-reduce | flops 16 | bytes 128 | tf_op jit(solution)/shard_map/pmax | solution.py:179
  1236.6 43.5 %all-reduce.17 = (f32[1024]{0:T(1024)S(1)}, f32[1024]{0:T(1024)S(1)}, f32[1024]{0:T(1024)S(1)}, f32[1024]{0:T(1024)S(1)}, f32[1024]{0:T(1024)S(1)}, /*index=5*/f...) all-reduce(f32[1024]{0:T(1024)S(1)} %get-tuple-element.268, ...), channel_id=2, replica_groups=mesh['dev'=32] {'dev'}, use_global_device_ids=true, to_apply=%region_19.20.clone | all-reduce | flops 12288 | bytes 98304
  1317.0 139.5 %reduce-scatter.11.cloned.1.call-done = f32[32,1024]{1,0:T(8,128)} async-done(((f32[1024,1024]{1,0:T(8,128)}), f32[32,1024]{1,0:T(8,128)}) %reduce-scatter.11.cloned.1.call-update) | async-done | bytes 131088 | tf_op jit(solution)/shard_map/reduce_scatter | solution.py:266
  1456.4 181.5 %reduce-scatter.17.cloned.1.call-done = f32[128,1024]{1,0:T(8,128)} async-done(((f32[4096,1024]{1,0:T(8,128)}), f32[128,1024]{1,0:T(8,128)}) %reduce-scatter.17.cloned.1.call-update) | async-done | bytes 524304 | tf_op jit(solution)/shard_map/reduce_scatter | solution.py:269
  1637.9 187.3 %reduce-scatter.15.cloned.1.call-done = f32[32,4096]{1,0:T(8,128)} async-done(((f32[1024,4096]{1,0:T(8,128)}), f32[32,4096]{1,0:T(8,128)}) %reduce-scatter.15.cloned.1.call-update) | async-done | bytes 524304 | tf_op jit(solution)/shard_map/reduce_scatter | solution.py:268
  (373 shorter events, 582.4 us)
Async XLA Ops:
  7.2 71.1 %all-gather.8.cloned.1.call-start = ((), (), s32[]{:S(2)}) async-start(), calls=%async_computation.6 | async-start | bytes 2162688 | tf_op jit(solution)/shard_map/all_gather | solution.py:106
  8.8 120.7 %all-gather.10.cloned.1.call-start = ((), (), s32[]{:S(2)}) async-start(), calls=%async_computation.7 | async-start | bytes 2162688 | tf_op jit(solution)/shard_map/all_gather | solution.py:107
  10.4 225.9 %all-gather.12.cloned.1.call-start = ((), (), s32[]{:S(2)}) async-start(), calls=%async_computation.8 | async-start | bytes 2162688 | tf_op jit(solution)/shard_map/all_gather | solution.py:105
  12.0 412.0 %all-gather.14.cloned.1.call-start = ((), (), s32[]{:S(2)}) async-start(), calls=%async_computation.9 | async-start | bytes 2162688 | tf_op jit(solution)/shard_map/all_gather | solution.py:108
  13.7 419.1 %all-gather.16.cloned.1.call-start = ((), (), s32[]{:S(2)}) async-start(), calls=%async_computation.10 | async-start | bytes 8650752 | tf_op jit(solution)/shard_map/all_gather | solution.py:109
  15.5 434.1 %all-gather.18.cloned.1.call-start = ((), (), s32[]{:S(2)}) async-start(), calls=%async_computation.11 | async-start | bytes 8650752 | tf_op jit(solution)/shard_map/all_gather | solution.py:110
  137.0 107.6 %collective-permute-start = (bf16[2,576,1024]{2,1,0:T(8,128)(2,1)}, bf16[2,576,1024]{2,1,0:T(8,128)(2,1)}, u32[]{:S(2)}, u32[]{:S(2)}) collective-permute-start(bf16[2,576,1024]{2,1,0:T(8,128)(2,1)} %get-tuple-element.340), channel_id=1, source_target_pairs={{0,1},{1,2},{2,3},{3,4},{4,5},{5,6},{6,7},{7,8},{8,9},{9,10},{10,1... | collective-permute-start | bytes 7077896 | tf_op jit(solution)/shard_map/ppermute | solution.py:25
  140.6 104.0 %collective-permute-start.1 = (bf16[2,576,1024]{2,1,0:T(8,128)(2,1)}, bf16[2,576,1024]{2,1,0:T(8,128)(2,1)}, u32[]{:S(2)}, u32[]{:S(2)}) collective-permute-start(bf16[2,576,1024]{2,1,0:T(8,128)(2,1)} %get-tuple-element.341), channel_id=1, source_target_pairs={{1,0},{2,1},{3,2},{4,3},{5,4},{6,5},{7,6},{8,7},{9,8},{10,9},{11,1... | collective-permute-start | bytes 7077896 | tf_op jit(solution)/shard_map/ppermute | solution.py:26
  142.0 94.3 %collective-permute-start.3 = (s32[576]{0:T(1024)S(1)}, s32[576]{0:T(1024)S(1)}, u32[]{:S(2)}, u32[]{:S(2)}) collective-permute-start(s32[576]{0:T(1024)S(1)} %get-tuple-element.344), channel_id=1, source_target_pairs={{1,0},{2,1},{3,2},{4,3},{5,4},{6,5},{7,6},{8,7},{9,8},{10,9},{11,1... | collective-permute-start | bytes 6920 | tf_op jit(solution)/shard_map/ppermute | solution.py:26
  143.3 93.0 %collective-permute-start.2 = (s32[576]{0:T(1024)S(1)}, s32[576]{0:T(1024)S(1)}, u32[]{:S(2)}, u32[]{:S(2)}) collective-permute-start(s32[576]{0:T(1024)S(1)} %get-tuple-element.345), channel_id=1, source_target_pairs={{0,1},{1,2},{2,3},{3,4},{4,5},{5,6},{6,7},{7,8},{8,9},{9,10},{10,1... | collective-permute-start | bytes 6920 | tf_op jit(solution)/shard_map/ppermute | solution.py:25
  147.7 1150.9 %reduce-scatter.13.cloned.1.call-start = ((), (), s32[]{:S(2)}) async-start(), calls=%async_computation.15 | async-start | bytes 4325376 | tf_op jit(solution)/shard_map/reduce_scatter | solution.py:267
  265.8 158.2 %copy-start.49 = (f32[1024]{0:T(1024)S(1)}, f32[1024]{0:T(1024)}, u32[]{:S(2)}) copy-start(f32[1024]{0:T(1024)} %convert_element_type.173) | copy-start | bytes 12292
  430.2 67.8 %copy-start.29 = (f32[1024]{0:T(1024)}, f32[1024]{0:T(1024)S(1)}, u32[]{:S(2)}) copy-start(f32[1024]{0:T(1024)S(1)} %broadcast_multiply_fusion.6) | copy-start | bytes 12292
  432.7 65.3 %copy-start.35 = (f32[1024]{0:T(1024)}, f32[1024]{0:T(1024)S(1)}, u32[]{:S(2)}) copy-start(f32[1024]{0:T(1024)S(1)} %add_rsqrt_fusion) | copy-start | bytes 12292
  509.9 788.7 %reduce-scatter.7.cloned.1.call-start = ((), (), s32[]{:S(2)}) async-start(), calls=%async_computation.12 | async-start | bytes 4325376 | tf_op jit(solution)/shard_map/reduce_scatter | solution.py:264
  1017.3 299.6 %reduce-scatter.9.cloned.1.call-start = ((), (), s32[]{:S(2)}) async-start(), calls=%async_computation.13 | async-start | bytes 4325376 | tf_op jit(solution)/shard_map/reduce_scatter | solution.py:265
  1026.4 10.0 collective-permute-start.4
  1031.0 6.5 collective-permute-start.5
  1056.8 399.6 %reduce-scatter.11.cloned.1.call-start = ((), (), s32[]{:S(2)}) async-start(), calls=%async_computation.14 | async-start | bytes 4325376 | tf_op jit(solution)/shard_map/reduce_scatter | solution.py:266
  1062.7 575.2 %reduce-scatter.17.cloned.1.call-start = ((), (), s32[]{:S(2)}) async-start(), calls=%async_computation.17 | async-start | bytes 17301504 | tf_op jit(solution)/shard_map/reduce_scatter | solution.py:269
  1081.3 744.0 %reduce-scatter.15.cloned.1.call-start = ((), (), s32[]{:S(2)}) async-start(), calls=%async_computation.16 | async-start | bytes 17301504 | tf_op jit(solution)/shard_map/reduce_scatter | solution.py:268
  1098.6 101.1 %copy-start.57 = (s32[16]{0:T(128)S(1)}, s32[16]{0:T(128)}, u32[]{:S(2)}) copy-start(s32[16]{0:T(128)} %param.44) | copy-start | bytes 196
  1098.6 101.2 %copy-start.23 = (f32[32,1024]{1,0:T(8,128)S(1)}, f32[32,1024]{1,0:T(8,128)}, u32[]{:S(2)}) copy-start(f32[32,1024]{1,0:T(8,128)} %param.32) | copy-start | bytes 393220
  1098.6 101.2 %copy-start.24 = (f32[32,1024]{1,0:T(8,128)S(1)}, f32[32,1024]{1,0:T(8,128)}, u32[]{:S(2)}) copy-start(f32[32,1024]{1,0:T(8,128)} %param.30) | copy-start | bytes 393220
  (73 other events, 685.2 us)
Sparse Core Ops, SparseCore 0:
  11.5 59.2 all-gather.7
  74.2 55.2 all-gather.9
  132.9 69.1 all-gather.11
  205.5 55.2 all-gather.13
  264.0 76.2 all-gather.15
  343.6 76.0 all-gather.17
  510.0 137.5 reduce-scatter.12
  1017.4 156.9 reduce-scatter.6
  1177.3 139.6 reduce-scatter.8
  1319.6 136.7 reduce-scatter.10
  1459.3 178.5 reduce-scatter.16
  1640.7 184.5 reduce-scatter.14
where the time goes:
time: 1840 us; the launch traced here: 1830 us
  waiting for transfers between devices  575 us (31%)
  matrix products  491 us (27%)
  blocking collectives  265 us (14%)
  other arithmetic  241 us (13%)
  local copies, waits for them, and re-layouts  221 us (12%)
    reduce_scatter x1, waiting for transfers between devices, local(): lax.psum_scatter(expand_mat_grad, 'dev', scatter_dimension=0, tiled=True)  187 us
    reduce_scatter x1, waiting for transfers between devices, local(): lax.psum_scatter(reduce_mat_grad, 'dev', scatter_dimension=0, tiled=True)  182 us
    reduce_scatter x1, waiting for transfers between devices, local(): lax.psum_scatter(value_mat_grad, 'dev', scatter_dimension=0, tiled=True)  139 us
    pmax x1, blocking collectives, local(): global_top = lax.pmax(jnp.max(block_top, axis=0), 'dev')  98.5 us
    convert_element_type x2, other arithmetic, attend_back(): score_grad = (prob_rows * (prob_grad - row_inner)).astype(bf16)  87.5 us
    unnamed x2, blocking collectives  86 us
    dot_general x4, matrix products, block_inputs(): jnp.einsum('qhd,khd->hqk', query_rows, key_rows, preferred_element_type=f32)  83.9 us
    all_gather x1, blocking collectives, local(): lax.all_gather(low_ebias, 'dev', axis=0, tiled=True)  80.5 us
  transfers between devices with their start and end apart: 18, of which 6 were waited for; matrix products, arithmetic and copies ran while one was open for 48% of the time, Pallas kernels for 0%

commit v1 on v0

v1 whole, which is shorter than its diff:
```python
import functools

import jax
import jax.numpy as jnp
from jax import lax
from jax.experimental import pallas as pl
from jax.experimental.pallas import tpu as pltpu
from jax.sharding import PartitionSpec as P

H = 16
HD = 64
LEN = 577
RIM = LEN - 1
PAIR = 2 * HD
QB = 256
KB = 256

NORM_EPS = 1e-05
CLIP_TAU = 3.0
GELU_COEF = 1.702
NEG_FILL = -1e30
SCALE = HD ** (-0.5)

bf16 = jnp.bfloat16
f32 = jnp.float32
NN = (((1,), (0,)), ((), ()))
NT = (((1,), (1,)), ((), ()))
TN = (((0,), (0,)), ((), ()))


def dot(lhs, rhs, dims):
    return lax.dot_general(lhs, rhs, dims, preferred_element_type=f32)


def norm_stats(values):
    centre = values - jnp.mean(values, axis=1, keepdims=True)
    inv_std = lax.rsqrt(jnp.mean(centre * centre, axis=1, keepdims=True) + NORM_EPS)
    return centre * inv_std, inv_std


def norm_back(grad_out, gain, normal, inv_std):
    scaled = grad_out * gain
    return inv_std * (
        scaled
        - jnp.mean(scaled, axis=1, keepdims=True)
        - normal * jnp.mean(scaled * normal, axis=1, keepdims=True)
    )


def column_sums(values):
    return jnp.sum(values.astype(f32), axis=0)


def two_heads(block):
    lane = lax.broadcasted_iota(jnp.int32, block.shape, 1)
    zero = jnp.zeros_like(block)
    return jnp.concatenate(
        [jnp.where(lane < HD, block, zero), jnp.where(lane >= HD, block, zero)], axis=0
    )


def fill_bias(bias_ref, key_ids_ref, query_ids_ref, block, low, count):
    def one(c, carry):
        start = pl.multiple_of(low + c * KB, 128)
        keys = key_ids_ref[pl.ds(start, KB), :]
        same = keys == query_ids_ref[...]
        bias_ref[block, pl.ds(pl.multiple_of(c * KB, KB), KB), :] = jnp.where(same, 0.0, NEG_FILL)
        return carry

    lax.fori_loop(0, count, one, 0)


def attend_kernel(
    low_ref, count_ref, key_ids_ref, query_ids_ref, q_ref, k_ref, v_ref, o_ref, wide_ref, lse_ref, top_ref, bias_ref
):
    pair, block = pl.program_id(0), pl.program_id(1)
    low, count = low_ref[block], count_ref[block]

    @pl.when(pair == 0)
    def _():
        fill_bias(bias_ref, key_ids_ref, query_ids_ref, block, low, count)

    queries = two_heads(q_ref[...])
    width = queries.shape[0]

    def step(c, carry):
        top, total, acc = carry
        start = pl.multiple_of(low + c * KB, 128)
        bias = bias_ref[block, pl.ds(pl.multiple_of(c * KB, KB), KB), :]
        scores = dot(k_ref[pl.ds(start, KB), :], queries, NT) * SCALE
        scores = scores + jnp.concatenate([bias, bias], axis=1)
        new_top = jnp.maximum(top, jnp.max(scores, axis=0, keepdims=True))
        weights = jnp.exp(scores - new_top)
        fade = jnp.exp(top - new_top)
        total = total * fade + jnp.sum(weights, axis=0, keepdims=True)
        acc = acc * fade + dot(v_ref[pl.ds(start, KB), :], weights.astype(bf16), TN)
        return new_top, total, acc

    start_top = jnp.full((1, width), NEG_FILL, f32)
    top, total, acc = lax.fori_loop(
        0, count, step, (start_top, jnp.zeros((1, width), f32), jnp.zeros((PAIR, width), f32))
    )
    mixed = acc / total
    half = width // 2
    joined = jnp.concatenate([mixed[:HD, :half], mixed[HD:, half:]], axis=0)
    joined = joined.T
    wide_ref[...] = joined
    o_ref[...] = joined.astype(bf16)
    lse_ref[0] = top + jnp.log(total)

    @pl.when(block == 0)
    def _():
        top_ref[0] = top

    @pl.when(block != 0)
    def _():
        top_ref[0] = jnp.maximum(top_ref[0], top)


def attend_back_kernel(
    low_ref,
    count_ref,
    key_ids_ref,
    query_ids_ref,
    q_ref,
    k_ref,
    v_ref,
    do_ref,
    o_ref,
    lse_ref,
    dq_ref,
    dk_ref,
    dv_ref,
    bias_ref,
    dk_acc,
    dv_acc,
):
    pair, block = pl.program_id(0), pl.program_id(1)
    low, count = low_ref[block], count_ref[block]

    @pl.when(pair == 0)
    def _():
        fill_bias(bias_ref, key_ids_ref, query_ids_ref, block, low, count)

    @pl.when(block == 0)
    def _():
        dk_acc[...] = jnp.zeros_like(dk_acc)
        dv_acc[...] = jnp.zeros_like(dv_acc)

    queries = two_heads(q_ref[...])
    grads = two_heads(do_ref[...])
    mixed = jnp.concatenate([o_ref[...], o_ref[...]], axis=0)
    inner = lax.dot_general(
        jnp.ones((8, PAIR), f32),
        grads.astype(f32) * mixed,
        NT,
        precision=lax.Precision.HIGHEST,
        preferred_element_type=f32,
    )[0:1]
    log_sum = lse_ref[0]
    width = queries.shape[0]

    def step(c, acc):
        start = pl.multiple_of(low + c * KB, 128)
        keys = k_ref[pl.ds(start, KB), :]
        bias = bias_ref[block, pl.ds(pl.multiple_of(c * KB, KB), KB), :]
        scores = dot(keys, queries, NT) * SCALE + jnp.concatenate([bias, bias], axis=1)
        probs = jnp.exp(scores - log_sum)
        prob_grad = dot(v_ref[pl.ds(start, KB), :], grads, NT)
        score_grad = (probs * (prob_grad - inner)).astype(bf16)
        dv_acc[pl.ds(start, KB), :] += dot(probs.astype(bf16), grads, NN)
        dk_acc[pl.ds(start, KB), :] += dot(score_grad, queries, NN)
        return acc + dot(keys, score_grad, TN)

    acc = lax.fori_loop(0, count, step, jnp.zeros((PAIR, width), f32))
    half = width // 2
    joined = jnp.concatenate([acc[:HD, :half], acc[HD:, half:]], axis=0) * SCALE
    dq_ref[...] = joined.T.astype(bf16)

    @pl.when(block == pl.num_programs(1) - 1)
    def _():
        dk_ref[...] = (dk_acc[...] * SCALE).astype(bf16)
        dv_ref[...] = dv_acc[...].astype(bf16)


def key_ranges(own_ids, near_ids, blocks):
    rows, near = own_ids.shape[0], near_ids.shape[0]
    size = rows // blocks
    place = jnp.arange(near, dtype=jnp.int32)[None, :]
    first = own_ids[0::size][:, None]
    last = own_ids[size - 1 :: size][:, None]
    low = jnp.min(jnp.where(near_ids[None, :] == first, place, near), axis=1)
    high = jnp.max(jnp.where(near_ids[None, :] == last, place, -1), axis=1) + 1
    low = low // 128 * 128
    count = (high - low + KB - 1) // KB
    low = jnp.minimum(low, near - count * KB)
    return low.astype(jnp.int32), count.astype(jnp.int32)


def attention_specs(rows, near, blocks):
    pairs = H // 2
    most = -(-(QB + 2 * RIM + 127) // KB) * KB
    assert most <= near and rows % QB == 0 and near % 128 == 0
    own = pl.BlockSpec((QB, PAIR), lambda p, b, *_: (b, p))
    base = [
        pl.BlockSpec((near, 1), lambda p, b, *_: (0, 0)),
        pl.BlockSpec((1, QB), lambda p, b, *_: (0, b)),
        own,
        pl.BlockSpec((near, PAIR), lambda p, b, *_: (0, p)),
        pl.BlockSpec((near, PAIR), lambda p, b, *_: (0, p + pairs)),
    ]
    row = pl.BlockSpec((1, 1, 2 * QB), lambda p, b, *_: (p, 0, b))
    bias = pltpu.VMEM((blocks, most, QB), f32)
    return pairs, own, base, row, bias


def attend(ranges, key_ids, query_ids, queries, near_kv):
    rows, near = queries.shape[0], near_kv.shape[0]
    blocks = rows // QB
    pairs, own, base, row, bias = attention_specs(rows, near, blocks)
    top = pl.BlockSpec((1, 1, 2 * QB), lambda p, b, *_: (p, 0, 0))
    return pl.pallas_call(
        attend_kernel,
        grid_spec=pltpu.PrefetchScalarGridSpec(
            num_scalar_prefetch=2,
            grid=(pairs, blocks),
            in_specs=base,
            out_specs=[own, own, row, top],
            scratch_shapes=[bias],
        ),
        out_shape=[
            jax.ShapeDtypeStruct(queries.shape, bf16),
            jax.ShapeDtypeStruct(queries.shape, f32),
            jax.ShapeDtypeStruct((pairs, 1, 2 * rows), f32),
            jax.ShapeDtypeStruct((pairs, 1, 2 * QB), f32),
        ],
        compiler_params=pltpu.CompilerParams(vmem_limit_bytes=56 << 20),
        name="attend",
    )(*ranges, key_ids, query_ids, queries, near_kv, near_kv)


def attend_back(ranges, key_ids, query_ids, queries, near_kv, mixed_grad, mixed, log_sums):
    rows, near = queries.shape[0], near_kv.shape[0]
    blocks = rows // QB
    pairs, own, base, row, bias = attention_specs(rows, near, blocks)
    wide = pl.BlockSpec((near, PAIR), lambda p, b, *_: (0, p))
    return pl.pallas_call(
        attend_back_kernel,
        grid_spec=pltpu.PrefetchScalarGridSpec(
            num_scalar_prefetch=2,
            grid=(pairs, blocks),
            in_specs=base + [own, own, row],
            out_specs=[own, wide, wide],
            scratch_shapes=[bias, pltpu.VMEM((near, PAIR), f32), pltpu.VMEM((near, PAIR), f32)],
        ),
        out_shape=[
            jax.ShapeDtypeStruct(queries.shape, bf16),
            jax.ShapeDtypeStruct((near, queries.shape[1]), bf16),
            jax.ShapeDtypeStruct((near, queries.shape[1]), bf16),
        ],
        compiler_params=pltpu.CompilerParams(vmem_limit_bytes=56 << 20),
        name="attend_back",
    )(*ranges, key_ids, query_ids, queries, near_kv, near_kv, mixed_grad, mixed, log_sums)


def mlp_kernel(
    a_ref, dz_ref, x_ref, rb_ref, eb_ref, we_ref, wr_ref,
    y_ref, da_ref, ebg_ref, sum_ref,
    act_ref, du_ref, rg_ref, eg_ref, sems,
):
    j = pl.program_id(0)
    rows, width = a_ref.shape
    tile = 256

    def copies(step):
        d, r, _ = rg_ref.shape
        g, e, _ = eg_ref.shape
        fold = pl.num_programs(0)
        return (
            pltpu.make_async_copy(rg_ref, sum_ref.at[pl.ds(step * d, d), pl.ds(0, r), :], sems.at[0]),
            pltpu.make_async_copy(eg_ref, sum_ref.at[:, pl.ds(r + step * e, e), :], sems.at[1]),
        )

    @pl.when(j == 0)
    def _():
        y_ref[...] = x_ref[...] + rb_ref[...]
        da_ref[...] = jnp.zeros_like(da_ref)

    ebg_ref[...] = jnp.zeros_like(ebg_ref)

    def by_rows(r, carry):
        at = pl.ds(pl.multiple_of(r * tile, tile), tile)
        we = we_ref[...].reshape(width, width)
        wr = wr_ref[...].reshape(width, width)
        hidden = dot(a_ref[at, :], we, NN) + eb_ref[...]
        back = dot(dz_ref[at, :], wr, NT)
        sigma = jax.nn.sigmoid(GELU_COEF * hidden)
        act = (hidden * sigma).astype(bf16)
        act_ref[at, :] = act
        du = (back * (sigma + GELU_COEF * hidden * sigma * (1.0 - sigma))).astype(bf16)
        du_ref[at, :] = du
        ebg_ref[...] += jnp.sum(du.astype(f32), axis=0, keepdims=True)
        y_ref[at, :] += dot(act, wr, NN)
        da_ref[at, :] += dot(du, we, NT)
        return carry

    lax.fori_loop(0, rows // tile, by_rows, 0)

    @pl.when(j > 0)
    def _():
        for copy in copies(j - 1):
            copy.wait()

    def by_columns(t, carry):
        at = pl.ds(pl.multiple_of(t * tile, tile), tile)
        rg = dot(act_ref[:, at], dz_ref[...], TN).astype(bf16)
        n = tile // rg_ref.shape[1]
        rg_ref[pl.ds(t * n, n)] = rg.reshape(n, rg_ref.shape[1], width)
        eg = dot(a_ref[:, at], du_ref[...], TN).astype(bf16)
        n = tile // eg_ref.shape[1]
        eg_ref[pl.ds(t * n, n)] = eg.reshape(n, eg_ref.shape[1], width)
        return carry

    lax.fori_loop(0, width // tile, by_columns, 0)
    for copy in copies(j):
        copy.start()

    @pl.when(j == pl.num_programs(0) - 1)
    def _():
        for copy in copies(j):
            copy.wait()


def mlp(normed, branch_grad, middle, bias_reduce, bias_expand, packed, sum_rows):
    rows, width = normed.shape
    ff = bias_expand.shape[1]
    fold = ff // width
    groups = packed.shape[0]
    each = width // groups
    whole = lambda j: (0, 0)
    one = pl.Buffered(1)
    return pl.pallas_call(
        mlp_kernel,
        grid=(fold,),
        in_specs=[
            pl.BlockSpec((rows, width), whole, pipeline_mode=one),
            pl.BlockSpec((rows, width), whole, pipeline_mode=one),
            pl.BlockSpec((rows, width), whole, pipeline_mode=one),
            pl.BlockSpec((1, width), whole),
            pl.BlockSpec((1, width), lambda j: (0, j)),
            pl.BlockSpec((groups, each, width), lambda j: (0, fold + j, 0)),
            pl.BlockSpec((groups // fold, fold * each, width), lambda j: (j, 0, 0)),
        ],
        out_specs=[
            pl.BlockSpec((rows, width), whole),
            pl.BlockSpec((rows, width), whole),
            pl.BlockSpec((1, width), lambda j: (0, j)),
            pl.BlockSpec(memory_space=pl.ANY),
        ],
        out_shape=[
            jax.ShapeDtypeStruct((rows, width), f32),
            jax.ShapeDtypeStruct((rows, width), f32),
            jax.ShapeDtypeStruct((1, ff), f32),
            jax.ShapeDtypeStruct((groups, sum_rows, width), bf16),
        ],
        scratch_shapes=[
            pltpu.VMEM((rows, width), bf16),
            pltpu.VMEM((rows, width), bf16),
            pltpu.VMEM((groups // fold, fold * each, width), bf16),
            pltpu.VMEM((groups, each, width), bf16),
            pltpu.SemaphoreType.DMA((2,)),
        ],
        compiler_params=pltpu.CompilerParams(vmem_limit_bytes=58 << 20),
        name="mlp",
    )(normed, branch_grad, middle, bias_reduce, bias_expand, packed, packed)


def out_back_kernel(ag_ref, mixed_ref, wo_ref, sum_in_ref, mg_ref, sum_ref, og_ref, sem):
    rows, width = ag_ref.shape
    tile = 256
    groups, each, _ = og_ref.shape

    def by_columns(t, carry):
        at = pl.ds(pl.multiple_of(t * tile, tile), tile)
        og = dot(mixed_ref[:, at], ag_ref[...], TN).astype(bf16)
        n = tile // each
        og_ref[pl.ds(t * n, n)] = og.reshape(n, each, width)
        return carry

    lax.fori_loop(0, width // tile, by_columns, 0)
    copy = pltpu.make_async_copy(og_ref, sum_ref.at[:, pl.ds(sum_ref.shape[1] - each, each), :], sem)
    copy.start()

    def by_rows(t, carry):
        at = pl.ds(pl.multiple_of(t * tile, tile), tile)
        mg_ref[at, :] = dot(ag_ref[at, :], wo_ref[...].reshape(width, width), NT).astype(bf16)
        return carry

    lax.fori_loop(0, rows // tile, by_rows, 0)
    copy.wait()


def out_back(attn_grad, mixed, packed, sums):
    rows, width = attn_grad.shape
    groups = packed.shape[0]
    each = width // groups
    last = sums.shape[1] // each - 1
    whole = lambda i: (0, 0)
    return pl.pallas_call(
        out_back_kernel,
        grid=(1,),
        in_specs=[
            pl.BlockSpec((rows, width), whole),
            pl.BlockSpec((rows, width), whole),
            pl.BlockSpec((groups, each, width), lambda i: (0, last, 0)),
            pl.BlockSpec(memory_space=pl.ANY),
        ],
        out_specs=[pl.BlockSpec((rows, width), whole), pl.BlockSpec(memory_space=pl.ANY)],
        out_shape=[
            jax.ShapeDtypeStruct((rows, width), bf16),
            jax.ShapeDtypeStruct(sums.shape, bf16),
        ],
        scratch_shapes=[pltpu.VMEM((groups, each, width), bf16), pltpu.SemaphoreType.DMA(())],
        input_output_aliases={3: 1},
        compiler_params=pltpu.CompilerParams(vmem_limit_bytes=56 << 20),
        name="out_back",
    )(attn_grad, mixed, packed, sums)


def qkv_kernel(a_ref, w_ref, bias_ref, q_ref, kv_ref):
    j = pl.program_id(0)
    near, width = a_ref.shape
    rows = q_ref.shape[0]
    rim = (near - rows) // 2

    @pl.when(j == 0)
    def _():
        def step(t, carry):
            source = pl.ds(pl.multiple_of(rim + t * 256, 8), 256)
            w = w_ref[...].reshape(width, width)
            q_ref[pl.ds(pl.multiple_of(t * 256, 256), 256), :] = (
                dot(a_ref[source, :], w, NN) + bias_ref[...]
            ).astype(bf16)
            return carry

        lax.fori_loop(0, rows // 256, step, 0)

    @pl.when(j > 0)
    def _():
        size = near // 8

        def step(t, carry):
            at = pl.ds(pl.multiple_of(t * size, 16), size)
            w = w_ref[...].reshape(width, width)
            kv_ref[at, :] = (dot(a_ref[at, :], w, NN) + bias_ref[...]).astype(bf16)
            return carry

        lax.fori_loop(0, near // size, step, 0)


def project(normed_near, packed, biases, rows):
    near, width = normed_near.shape
    groups = packed.shape[0]
    each = width // groups
    return pl.pallas_call(
        qkv_kernel,
        grid=(3,),
        in_specs=[
            pl.BlockSpec((near, width), lambda j: (0, 0)),
            pl.BlockSpec((groups, each, width), lambda j: (0, j, 0)),
            pl.BlockSpec((1, width), lambda j: (0, j)),
        ],
        out_specs=[
            pl.BlockSpec((rows, width), lambda j: (0, 0)),
            pl.BlockSpec((near, width), lambda j: (0, jnp.maximum(j - 1, 0))),
        ],
        out_shape=[
            jax.ShapeDtypeStruct((rows, width), bf16),
            jax.ShapeDtypeStruct((near, 2 * width), bf16),
        ],
        compiler_params=pltpu.CompilerParams(vmem_limit_bytes=56 << 20),
        name="qkv",
    )(normed_near, packed, biases)


def qkv_grads_kernel(me_ref, a_ref, dq_ref, dk_ref, dv_ref, keep_ref, send_ref):
    j = pl.program_id(0)
    near, width = a_ref.shape
    rows = dq_ref.shape[0]
    rim = (near - rows) // 2
    tile = 256
    half, each, _ = keep_ref.shape
    n = tile // each

    def fill(grad_ref, source):
        def step(t, carry):
            at = pl.ds(pl.multiple_of(t * tile, tile), tile)
            out = dot(a_ref[source, at], grad_ref[...], TN).astype(bf16)
            for i in range(n):
                place = (t * n + i) ^ me_ref[0]
                spot, bit = 0, half
                while bit:
                    spot = spot + (place & 1) * bit
                    place, bit = place >> 1, bit >> 1
                block = out[i * each : (i + 1) * each]

                @pl.when(spot < half)
                def _():
                    keep_ref[spot] = block

                @pl.when(spot >= half)
                def _():
                    send_ref[spot - half] = block

            return carry

        lax.fori_loop(0, width // tile, step, 0)

    @pl.when(j == 0)
    def _():
        fill(dq_ref, slice(rim, rim + rows))

    @pl.when(j == 1)
    def _():
        fill(dk_ref, slice(0, near))

    @pl.when(j == 2)
    def _():
        fill(dv_ref, slice(0, near))


def qkv_grads(normed_near, query_grad, key_near, value_near, groups, place):
    near, width = normed_near.shape
    rows = query_grad.shape[0]
    each = width // groups
    whole = lambda j, *_: (0, 0)
    half = jax.ShapeDtypeStruct((groups // 2, 3 * each, width), bf16)
    out = pl.BlockSpec((groups // 2, each, width), lambda j, *_: (0, j, 0))
    return pl.pallas_call(
        qkv_grads_kernel,
        grid_spec=pltpu.PrefetchScalarGridSpec(
            num_scalar_prefetch=1,
            grid=(3,),
            in_specs=[
                pl.BlockSpec((near, width), whole),
                pl.BlockSpec((rows, width), whole),
                pl.BlockSpec((near, width), whole),
                pl.BlockSpec((near, width), whole),
            ],
            out_specs=[out, out],
        ),
        out_shape=[half, half],
        compiler_params=pltpu.CompilerParams(vmem_limit_bytes=56 << 20),
        name="qkv_grads",
    )(jnp.full((1,), place, jnp.int32), normed_near, query_grad, key_near, value_near)


def plus(a, b):
    return (a.astype(f32) + b.astype(f32)).astype(bf16)


def swap(value, bit):
    peers = lax.axis_size("dev")
    return lax.ppermute(value, "dev", [(i, i ^ bit) for i in range(peers)])


def halving(keep, send):
    _, rows, width = keep.shape
    half = rows // 2
    other = swap(send, 1).reshape(2, 2, 4, rows, width)
    keep = keep.reshape(2, 2, 4, rows, width)
    a, b = slice(0, half), slice(half, rows)
    from_x = swap(plus(keep[1, :, :, a], other[1, :, :, a]), 2)
    from_y = swap(plus(keep[:, 1, :, b], other[:, 1, :, b]), 4)
    keep_x = plus(keep[0, :, :, a], other[0, :, :, a])
    keep_y = plus(keep[:, 0, :, b], other[:, 0, :, b])
    second_y = swap(plus(keep_x[1], from_x[1]), 4)
    second_x = swap(plus(keep_y[1], from_y[1]), 2)
    keep_x = plus(keep_x[0], from_x[0])
    keep_y = plus(keep_y[0], from_y[0])
    send = jnp.concatenate([plus(keep_x[2:], second_y[2:]), plus(keep_y[2:], second_x[2:])], axis=1)
    low = swap(send, 8)
    keep = jnp.concatenate([plus(keep_x[:2], second_y[:2]), plus(keep_y[:2], second_x[:2])], axis=1)
    last = swap(plus(keep[1], low[1]), 16)
    return plus(keep[0], low[0]).astype(f32) + last.astype(f32)


def normed_grad_kernel(dq_ref, dkv_ref, w_ref, out_ref):
    j = pl.program_id(0)
    rows, width = out_ref.shape

    def step(t, carry):
        at = pl.ds(pl.multiple_of(t * 256, 256), 256)
        w = w_ref[...].reshape(width, width)

        @pl.when(j == 0)
        def _():
            out_ref[at, :] = dot(dq_ref[at, :], w, NT)

        @pl.when(j > 0)
        def _():
            out_ref[at, :] += dot(dkv_ref[at, :], w, NT)

        return carry

    lax.fori_loop(0, rows // 256, step, 0)


def project_back(query_grad, kv_grad, packed):
    rows, width = query_grad.shape
    groups = packed.shape[0]
    each = width // groups
    return pl.pallas_call(
        normed_grad_kernel,
        grid=(3,),
        in_specs=[
            pl.BlockSpec((rows, width), lambda j: (0, 0)),
            pl.BlockSpec((rows, width), lambda j: (0, jnp.maximum(j - 1, 0))),
            pl.BlockSpec((groups, each, width), lambda j: (0, j, 0)),
        ],
        out_specs=pl.BlockSpec((rows, width), lambda j: (0, 0)),
        out_shape=jax.ShapeDtypeStruct((rows, width), f32),
        compiler_params=pltpu.CompilerParams(vmem_limit_bytes=56 << 20),
        name="normed_grad",
    )(query_grad, kv_grad, packed)


def gather(value, segments, groups):
    peers = lax.axis_size("dev")
    rows, width = value.shape
    whole = lax.all_gather(value, "dev", axis=0, tiled=True)
    sub = peers // groups
    if sub == 1:
        return whole.reshape(groups, rows, width)
    whole = whole.reshape(groups, sub, rows, width)
    parts, at = [], 0
    for size in segments:
        parts.append(whole[:, :, at : at + size].reshape(groups, sub * size, width))
        at += size
    return jnp.concatenate(parts, axis=1)


def scatter(value, segments):
    peers = lax.axis_size("dev")
    groups, rows, width = value.shape
    sub = peers // groups
    if sub > 1:
        parts, at = [], 0
        for size in segments:
            cut = value[:, at : at + sub * size]
            parts.append(cut.reshape(groups, sub, size, width))
            at += sub * size
        value = jnp.concatenate(parts, axis=2)
    value = value.reshape(peers * sum(segments), width)
    return lax.psum_scatter(value, "dev", scatter_dimension=0, tiled=True)


def spread(vector, width):
    peers, me = lax.axis_size("dev"), lax.axis_index("dev")
    size = vector.shape[0]
    place = jnp.arange(peers * size, dtype=jnp.int32) // size
    full = jnp.where(place == me, jnp.tile(vector, peers), jnp.zeros((), vector.dtype))
    return full.reshape(-1, width)


def local(
    tokens_in,
    attn_gain,
    attn_bias,
    query_mat,
    query_bias,
    key_mat,
    value_mat,
    value_bias,
    output_mat,
    output_bias,
    mlp_gain,
    mlp_bias,
    expand_mat,
    expand_bias,
    reduce_mat,
    reduce_bias,
    image_ids,
    clip_flags,
    out_grad,
):
    peers, me = lax.axis_size("dev"), lax.axis_index("dev")
    rows, width = tokens_in.shape
    part = query_mat.shape[0]
    ff = expand_mat.shape[1]
    fold = ff // width
    groups = min(peers, 32)
    sub = peers // groups

    small = jnp.concatenate(
        [
            spread(v.astype(bf16), width)
            for v in (
                attn_gain,
                attn_bias,
                query_bias,
                value_bias,
                output_bias,
                mlp_gain,
                mlp_bias,
                reduce_bias,
            )
        ]
    )
    packed_one = jnp.concatenate([query_mat.astype(bf16), key_mat.astype(bf16), value_mat.astype(bf16), small])
    first = gather(packed_one, [part] * 3 + [8], groups)

    up = [(i, i + 1) for i in range(peers - 1)]
    down = [(i + 1, i) for i in range(peers - 1)]
    normal_one, inv_one = norm_stats(tokens_in)
    normal_low = normal_one.astype(bf16)
    before = lax.ppermute(normal_low[rows - RIM :], "dev", up)
    after = lax.ppermute(normal_low[:RIM], "dev", down)
    own_ids = image_ids + 1
    ids_before = lax.ppermute(own_ids[rows - RIM :], "dev", up)
    ids_after = lax.ppermute(own_ids[:RIM], "dev", down)
    near_ids = jnp.concatenate([ids_before, own_ids, ids_after])
    ranges = key_ranges(own_ids, near_ids, rows // QB)
    key_ids, query_ids = near_ids[:, None], own_ids[None, :]

    expand_low = expand_mat.astype(bf16)
    second = jnp.concatenate(
        [reduce_mat.astype(bf16)]
        + [expand_low[:, i * width : (i + 1) * width] for i in range(fold)]
        + [output_mat.astype(bf16), spread(expand_bias.astype(bf16), width), jnp.zeros((8 - fold, width), bf16)]
    )
    second, before, after = lax.optimization_barrier((second, before, after))
    second = gather(second, [fold * part] + [part] * (fold + 1) + [8], groups)

    vectors = jnp.sum(first[:, groups * 0 + 3 * part * sub :].reshape(groups * sub, 8, width).astype(f32), axis=0)
    (gain_one, bias_one, bias_query, bias_value, bias_output, gain_two, bias_two, bias_reduce) = [
        vectors[i : i + 1] for i in range(8)
    ]

    normed_near = jnp.concatenate(
        [(v.astype(f32) * gain_one + bias_one).astype(bf16) for v in (before, normal_one, after)], axis=0
    )
    bias_qkv = jnp.concatenate([bias_query, jnp.zeros_like(bias_value), bias_value], axis=1)
    queries, near_kv = project(normed_near, first, bias_qkv, rows)
    mixed, mixed_wide, log_sums, tops = attend(ranges, key_ids, query_ids, queries, near_kv)
    head_top = jnp.max(tops.reshape(H, QB), axis=1)

    tail = second[:, (2 * fold + 1) * part * sub :].reshape(groups * sub, 8, width)
    bias_expand = jnp.sum(tail.astype(f32), axis=0)[:fold].reshape(1, ff)
    w_output = second[:, 2 * fold * part * sub : (2 * fold + 1) * part * sub].reshape(width, width)
    middle = tokens_in + dot(mixed, w_output, NN) + bias_output
    normal_two, inv_two = norm_stats(middle)
    normed_two = (normal_two * gain_two + bias_two).astype(bf16)
    branch_grad = out_grad.astype(bf16)
    block_out, normed_two_grad, expand_bias_grad, sums = mlp(
        normed_two, branch_grad, middle, bias_reduce, bias_expand, second, (2 * fold + 1) * width // groups
    )
    reduce_bias_grad = column_sums(branch_grad)
    mlp_gain_grad = jnp.sum(normed_two_grad * normal_two, axis=0)
    mlp_bias_grad = jnp.sum(normed_two_grad, axis=0)
    middle_grad = out_grad + norm_back(normed_two_grad, gain_two, normal_two, inv_two)
    attn_grad = middle_grad.astype(bf16)
    output_bias_grad = column_sums(attn_grad)
    mixed_grad, sums = out_back(attn_grad, mixed, second, sums)
    first_sum = scatter(sums, [fold * part] + [part] * (fold + 1))

    query_grad, key_near, value_near = attend_back(
        ranges, key_ids, query_ids, queries, near_kv, mixed_grad, mixed_wide, log_sums
    )
    halves = qkv_grads(normed_near, query_grad, key_near, value_near, groups, me if peers == 32 else 0)
    if peers == 32:
        second_sum = halving(*halves)
    else:
        order = [int(f"{i:05b}"[::-1], 2) for i in range(groups)]
        joined = jnp.concatenate(halves, axis=0)
        second_sum = scatter(jnp.stack([joined[i] for i in order]), [part] * 3)
    outgoing = jnp.concatenate([key_near, value_near], axis=1)
    from_next = lax.ppermute(outgoing[:RIM], "dev", down)
    from_prev = lax.ppermute(outgoing[RIM + rows :], "dev", up)
    own = outgoing[RIM : RIM + rows].astype(f32)
    own = own + jnp.pad(from_prev.astype(f32), ((0, rows - RIM), (0, 0)))
    own = own + jnp.pad(from_next.astype(f32), ((rows - RIM, 0), (0, 0)))
    kv_grad = own.astype(bf16)
    query_bias_grad = column_sums(query_grad)
    value_bias_grad = column_sums(value_near)
    normed_grad = project_back(query_grad, kv_grad, first)
    attn_gain_grad = jnp.sum(normed_grad * normal_one, axis=0)
    attn_bias_grad = jnp.sum(normed_grad, axis=0)
    tokens_grad = middle_grad + norm_back(normed_grad, gain_one, normal_one, inv_one)

    totals = jnp.stack(
        [
            attn_gain_grad,
            attn_bias_grad,
            query_bias_grad,
            value_bias_grad,
            output_bias_grad,
            mlp_gain_grad,
            mlp_bias_grad,
            reduce_bias_grad,
        ]
    )
    totals = jnp.concatenate(
        [totals, expand_bias_grad.reshape(fold, width), jnp.pad(head_top, (0, width - H))[None]]
    )
    is_top = jnp.arange(totals.shape[0])[:, None] == totals.shape[0] - 1
    bit = 1
    while bit < peers:
        other = lax.ppermute(totals, "dev", [(i, i ^ bit) for i in range(peers)])
        totals = jnp.where(is_top, jnp.maximum(totals, other), totals + other)
        bit *= 2
    mine = lax.dynamic_slice_in_dim(totals[:8], me * part, part, 1)
    expand_mine = lax.dynamic_slice_in_dim(totals[8 : 8 + fold].reshape(-1), me * part * fold, part * fold, 0)
    global_top = totals[-1, :H]

    first_sum = first_sum.astype(f32)
    second_sum = second_sum.astype(f32)
    expand_out = jnp.concatenate(
        [first_sum[(fold + i) * part : (fold + i + 1) * part] for i in range(fold)], axis=1
    )
    ratio = CLIP_TAU / jnp.maximum(global_top, CLIP_TAU)
    factor = jnp.where(clip_flags == 1, jnp.sqrt(ratio), 1.0)
    by_column = jnp.repeat(factor, HD)
    return (
        block_out,
        tokens_grad,
        query_mat * by_column[None, :],
        key_mat * by_column[None, :],
        mine[0],
        mine[1],
        second_sum[:part],
        mine[2],
        second_sum[part : 2 * part],
        second_sum[2 * part : 3 * part],
        mine[3],
        first_sum[2 * fold * part :],
        mine[4],
        mine[5],
        mine[6],
        expand_out,
        expand_mine,
        first_sum[: fold * part],
        mine[7],
    )


def solution(mesh):
    split, both = P("dev"), P("dev", None)
    mat = both
    in_specs = (
        mat, split, split, mat, split, mat, mat, split, mat, split, split, split, mat, split, mat, split,
        split, P(), mat,
    )
    out_specs = (
        mat, mat, mat, mat, split, split, mat, split, mat, mat, split, mat, split, split, split, mat,
        split, mat, split,
    )
    return jax.shard_map(local, mesh=mesh, in_specs=in_specs, out_specs=out_specs, check_vma=False)
```

time: 1840 us -> 644 us (0.35)
  matrix products: 491 us -> 4.05 us
  waiting for transfers between devices: 575 us -> 151 us
  Pallas kernels: 0 us -> 282 us
  blocking collectives: 265 us -> 0 us
  local copies, waits for them, and re-layouts: 221 us -> 37.4 us
  other arithmetic: 241 us -> 66.3 us
  starting transfers between devices: 16.3 us -> 87.3 us
    reduce_scatter x6 -> x1, waiting for transfers between devices: 527 us -> 0.01 us  [scatter(): return lax.psum_scatter(value, 'dev', scatter_dimension=0, tiled=True)]
    dot_general x32 -> x1, matrix products: 491 us -> 4.05 us  [dot(): return lax.dot_general(lhs, rhs, dims, preferred_element_type=f32)]
    pallas_call x0 -> x7, Pallas kernels: none -> 282 us  [the longest x1 77.2 us: attend_back(): pl.pallas_call(attend_back_kernel, grid_spec=pltpu.PrefetchScalarGridSpec...]
    pmax x1 -> x0, blocking collectives: 98.5 us -> none  [local(): global_top = lax.pmax(jnp.max(block_top, axis=0), 'dev')]
    unnamed x2 -> x0, blocking collectives: 86 us -> none
    all_gather x1 -> x0, blocking collectives: 80.5 us -> none  [local(): lax.all_gather(low_ebias, 'dev', axis=0, tiled=True)]
    convert_element_type x26, other arithmetic: 106 us -> 27.2 us  [the longest x1 6.29 us: local(): kv_grad = own.astype(bf16)]
    ppermute x6 -> x18, starting transfers between devices: 15.8 us -> 87.2 us  [the longest x5 46.2 us: local(): other = lax.ppermute(totals, 'dev', [(i, i ^ bit) for i in range(peers)])]
  transfers between devices with their start and end apart: 18 -> 21, of which waited for: 6 -> 12; matrix products, arithmetic and copies ran while one was open for 48% -> 10% of each run, Pallas kernels for 0% -> 31%
where the time goes in v1:
time: 644 us; the launch traced here: 642 us
  Pallas kernels  282 us (44%)
  waiting for transfers between devices  151 us (23%)
  starting transfers between devices  87.3 us (14%)
  other arithmetic  66.3 us (10%)
  local copies, waits for them, and re-layouts  37.4 us (6%)
  between operations  14.4 us (2%)
    all_gather x2, waiting for transfers between devices, gather(): whole = lax.all_gather(value, 'dev', axis=0, tiled=True)  95.9 us
    pallas_call x1, Pallas kernels, attend_back(): pl.pallas_call(attend_back_kernel, grid_spec=pltpu.PrefetchScalarGridSpec...  77.2 us
    pallas_call x1, Pallas kernels, mlp(): pl.pallas_call(mlp_kernel, grid=(fold,), in_specs=[pl.BlockSpec((rows, wi...  71.6 us
    pallas_call x1, Pallas kernels, attend(): pl.pallas_call(attend_kernel, grid_spec=pltpu.PrefetchScalarGridSpec(num_...  63 us
    ppermute x5, starting transfers between devices, local(): other = lax.ppermute(totals, 'dev', [(i, i ^ bit) for i in range(peers)])  46.2 us
    ppermute x7, waiting for transfers between devices, swap(): return lax.ppermute(value, 'dev', [(i, i ^ bit) for i in range(peers)])  40.8 us
    pallas_call x1, Pallas kernels, qkv_grads(): pl.pallas_call(qkv_grads_kernel, grid_spec=pltpu.PrefetchScalarGridSpec(n...  24 us
    pallas_call x1, Pallas kernels, project(): pl.pallas_call(qkv_kernel, grid=(3,), in_specs=[pl.BlockSpec((near, width...  20.6 us
  transfers between devices with their start and end apart: 21, of which 12 were waited for; matrix products, arithmetic and copies ran while one was open for 10% of the time, Pallas kernels for 31%

profile of v1, /device:TPU:0, one launch (start us, length us, event | category | flops | bytes accessed | tf_op | source)
XLA Modules:
  0.0 642.4 jit_solution(7805292183665575601)
XLA Ops:
  23.9 69.1 %all-gather.3.cloned.1.call-done = bf16[3328,1024]{1,0:T(8,128)(2,1)} async-done(((bf16[104,1024]{1,0:T(8,128)(2,1)}), bf16[3328,1024]{1,0:T(8,128)(2,1)}) %all-gather.3.cloned.1.call-update) | async-done | bytes 6815760 | tf_op jit(solution)/shard_map/all_gather | solution.py:631
  100.7 4.0 collective-permute-start.2
  107.5 9.4 %concatenate.31 = bf16[296,1024]{1,0:T(8,128)(2,1)} concatenate(bf16[128,1024]{1,0:T(8,128)(2,1)S(1)} %convert_element_type.306, bf16[32,1024]{1,0:T(8,128)(2,1)} %get-tuple-element.105, bf16[32,1024]{1,0:T(8,128)(2,1)} %get-tuple-element.104, bf16[32,1024]{1,0:T(8,128)(2,1)} %get-tuple-element.103, bf16[32,1024]{1,0:T(8,128)(2,1)} %get-tuple-element.102, ...), dimensions={0} | concatenate | bytes 1212416 | tf_op jit(solution)/shard_map/concatenate | solution.py:727
  119.0 16.0 %collective-permute-start = (s32[576]{0:T(1024)S(1)}, s32[576]{0:T(1024)S(1)}, u32[]{:S(2)}, u32[]{:S(2)}) collective-permute-start(s32[576]{0:T(1024)S(1)} %get-tuple-element.127), channel_id=1, source_target_pairs={{0,1},{1,2},{2,3},{3,4},{4,5},{5,6},{6,7},{7,8},{8,9},{9,10},{10,1... | collective-permute-start | bytes 6920 | tf_op jit(solution)/shard_map/ppermute | solution.py:720
  135.1 4.0 convert_reduce_fusion.1
  146.7 20.6 %qkv.1 = (bf16[1024,1024]{1,0:T(8,128)(2,1)}, bf16[2176,2048]{1,0:T(8,128)(2,1)}) custom-call(bf16[2176,1024]{1,0:T(8,128)(2,1)} %pad_maximum_fusion.a_ref, bf16[32,104,1024]{2,1,0:T(8,128)(2,1)} %bitcast.118, f32[1,3072]{1,0:T(1,128)} %pad_maximum_fusion.4.bias_ref), custom_call_target="tpu_custom_call" | custom-call | tf_op jit(solution)/shard_map/qkv/pallas_call | solution.py:465
  167.3 63.0 %attend.1 = (bf16[1024,1024]{1,0:T(8,128)(2,1)}, f32[1024,1024]{1,0:T(8,128)}, f32[8,1,2048]{2,1,0:T(1,128)}, f32[8,1,512]{2,1,0:T(1,128)}) custom-call(s32[4]{0:T(128)} %get-tuple-element.74.low_ref, s32[4]{0:T(128)} %get-tuple-element.75.count_ref, s32[2176,1]{1,0:T(8,128)} %broadcast_in_dim.114.key_ids_ref, s32[1,1024]{1,0:T(1,128)} %bitcast.123, ...), custom_call_target="tpu_custom_call" | custom-call | tf_op jit(solution)/shard_map/attend/pallas_call | solution.py:222
  230.3 26.8 %all-gather.5.cloned.1.call-done = bf16[9472,1024]{1,0:T(8,128)(2,1)} async-done(((bf16[296,1024]{1,0:T(8,128)(2,1)}), bf16[9472,1024]{1,0:T(8,128)(2,1)}) %all-gather.5.cloned.1.call-update) | async-done | bytes 19398672 | tf_op jit(solution)/shard_map/all_gather | solution.py:631
  261.1 4.0 fusion.33
  267.8 71.6 %mlp.1 = (f32[1024,1024]{1,0:T(8,128)}, f32[1024,1024]{1,0:T(8,128)}, f32[1,4096]{1,0:T(1,128)}, bf16[32,288,1024]{2,1,0:T(8,128)(2,1)}) custom-call(bf16[1024,1024]{1,0:T(8,128)(2,1)} %add_convert_fusion.1.a_ref, bf16[1024,1024]{1,0:T(8,128)(2,1)} %get-tuple-element.70.dz_ref, f32[1024,1024]{1,0:T(8,128)} %copy-done.3, ...), custom_call_target="tpu_custom_call" | custom-call | tf_op jit(solution)/shard_map/mlp/pallas_call | solution.py:342
  347.5 10.2 %out_back.1 = (bf16[1024,1024]{1,0:T(8,128)(2,1)}, bf16[32,288,1024]{2,1,0:T(8,128)(2,1)}) custom-call(bf16[1024,1024]{1,0:T(8,128)(2,1)} %get-tuple-element.72.ag_ref, bf16[1024,1024]{1,0:T(8,128)(2,1)} %get-tuple-element.43.mixed_ref, bf16[32,296,1024]{2,1,0:T(8,128)(2,1)} %bitcast.115, ...), custom_call_target="tpu_custom_call", output_to_operand_aliasing={{1}: (3, {})} | custom-call | tf_op jit(solution)/shard_map/out_back/pallas_call | solution.py:409
  357.8 77.2 %attend_back.1 = (bf16[1024,1024]{1,0:T(8,128)(2,1)}, bf16[2176,1024]{1,0:T(8,128)(2,1)}, bf16[2176,1024]{1,0:T(8,128)(2,1)}) custom-call(s32[4]{0:T(128)} %get-tuple-element.74.low_ref, s32[4]{0:T(128)} %get-tuple-element.75.count_ref, s32[2176,1]{1,0:T(8,128)} %broadcast_in_dim.114.key_ids_ref, s32[1,1024]{1,0:T(1,128)} %bitcast.124, ...), custom_call_target="tpu_custom_call" | custom-call | tf_op jit(solution)/shard_map/attend_back/pallas_call | solution.py:247
  444.5 11.9 %collective-permute-start.4 = (bf16[576,2048]{1,0:T(8,128)(2,1)}, bf16[576,2048]{1,0:T(8,128)(2,1)}, u32[]{:S(2)}, u32[]{:S(2)}) collective-permute-start(bf16[576,2048]{1,0:T(8,128)(2,1)} %get-tuple-element.76), channel_id=1, source_target_pairs={{0,1},{1,2},{2,3},{3,4},{4,5},{5,6},{6,7},{7,8},{8,9},{9,10},{10,1... | collective-permute-start | bytes 7077896 | tf_op jit(solution)/shard_map/ppermute | solution.py:779
  457.9 24.0 %qkv_grads.1 = (bf16[16,96,1024]{2,1,0:T(8,128)(2,1)}, bf16[16,96,1024]{2,1,0:T(8,128)(2,1)}) custom-call(s32[1]{0:T(128)} %bitcast.22.me_ref, bf16[2176,1024]{1,0:T(8,128)(2,1)} %pad_maximum_fusion.a_ref, bf16[1024,1024]{1,0:T(8,128)(2,1)} %get-tuple-element.51.dq_ref, bf16[2176,1024]{1,0:T(8,128)(2,1)} %get-tuple-element.52.dk_ref, ...), custom_call_target="tpu_custom_call" | custom-call | tf_op jit(solution)/shard_map/qkv_grads/pallas_call | solution.py:539
  487.5 6.3 add_convert_fusion.dkv_ref
  493.8 15.6 %normed_grad.1 = f32[1024,1024]{1,0:T(8,128)} custom-call(bf16[1024,1024]{1,0:T(8,128)(2,1)} %get-tuple-element.51.dq_ref, bf16[1024,2048]{1,0:T(8,128)(2,1)} %add_convert_fusion.dkv_ref, bf16[32,104,1024]{2,1,0:T(8,128)(2,1)} %bitcast.119), custom_call_target="tpu_custom_call" | custom-call | tf_op jit(solution)/shard_map/normed_grad/pallas_call | solution.py:613
  513.2 35.7 %collective-permute-start.6 = (f32[13,1024]{1,0:T(8,128)S(1)}, f32[13,1024]{1,0:T(8,128)S(1)}, u32[]{:S(2)}, u32[]{:S(2)}) collective-permute-start(f32[13,1024]{1,0:T(8,128)S(1)} %concatenate.36), channel_id=1, source_target_pairs={{0,1},{1,0},{2,3},{3,2},{4,5},{5,4},{6,7},{7,6},{8,9},{9,8},{10,11... | collective-permute-start | bytes 159752 | tf_op jit(solution)/shard_map/ppermute | solution.py:809
  560.4 6.7 %collective-permute-done.9 = f32[13,1024]{1,0:T(8,128)S(1)} collective-permute-done((f32[13,1024]{1,0:T(8,128)S(1)}, f32[13,1024]{1,0:T(8,128)S(1)}, u32[]{:S(2)}, u32[]{:S(2)}) %collective-permute-start.9) | collective-permute-done | bytes 53280 | tf_op jit(solution)/shard_map/ppermute | solution.py:809
  567.2 6.6 %collective-permute-start.10 = (f32[13,1024]{1,0:T(8,128)S(1)}, f32[13,1024]{1,0:T(8,128)S(1)}, u32[]{:S(2)}, u32[]{:S(2)}) collective-permute-start(f32[13,1024]{1,0:T(8,128)S(1)} %add_select_fusion.1), channel_id=1, source_target_pairs={{0,16},{1,17},{2,18},{3,19},{4,20},{5,21},{6,22},{7,23},{8,24},{9,... | collective-permute-start | bytes 159752 | tf_op jit(solution)/shard_map/ppermute | solution.py:809
  580.9 4.3 multiply_add_fusion
  585.3 12.4 %collective-permute-done.14 = bf16[2,4,48,1024]{3,2,1,0:T(8,128)(2,1)S(1)} collective-permute-done((bf16[2,4,48,1024]{3,2,1,0:T(8,128)(2,1)S(1)}, bf16[2,4,48,1024]{3,2,1,0:T(8,128)(2,1)S(1)}, u32[]{:S(2)}, u32[]{:S(2)}) %collective-permute-start.14) | collective-permute-done | bytes 786464 | tf_op jit(solution)/shard_map/ppermute | solution.py:564
  598.1 6.4 collective-permute-done.12
  614.5 8.3 %collective-permute-done.16 = bf16[2,96,1024]{2,1,0:T(8,128)(2,1)S(1)} collective-permute-done((bf16[2,96,1024]{2,1,0:T(8,128)(2,1)S(1)}, bf16[2,96,1024]{2,1,0:T(8,128)(2,1)S(1)}, u32[]{:S(2)}, u32[]{:S(2)}) %collective-permute-start.16) | collective-permute-done | bytes 393248 | tf_op jit(solution)/shard_map/ppermute | solution.py:564
  623.9 6.9 %collective-permute-done.17 = bf16[96,1024]{1,0:T(8,128)(2,1)S(1)} collective-permute-done((bf16[96,1024]{1,0:T(8,128)(2,1)S(1)}, bf16[96,1024]{1,0:T(8,128)(2,1)S(1)}, u32[]{:S(2)}, u32[]{:S(2)}) %collective-permute-start.17) | collective-permute-done | bytes 196640 | tf_op jit(solution)/shard_map/ppermute | solution.py:564
  (207 shorter events, 107.0 us)
Async XLA Ops:
  7.2 85.8 %all-gather.3.cloned.1.call-start = ((), (), s32[]{:S(2)}) async-start(), calls=%async_computation.1 | async-start | bytes 7028736 | tf_op jit(solution)/shard_map/all_gather | solution.py:631
  18.7 238.4 %all-gather.5.cloned.1.call-start = ((), (), s32[]{:S(2)}) async-start(), calls=%async_computation.2 | async-start | bytes 20004864 | tf_op jit(solution)/shard_map/all_gather | solution.py:631
  99.5 17.4 %collective-permute-start.3 = (bf16[576,1024]{1,0:T(8,128)(2,1)}, bf16[576,1024]{1,0:T(8,128)(2,1)S(1)}, u32[]{:S(2)}, u32[]{:S(2)}) collective-permute-start(bf16[576,1024]{1,0:T(8,128)(2,1)} %get-tuple-element.84), channel_id=1, source_target_pairs={{1,0},{2,1},{3,2},{4,3},{5,4},{6,5},{7,6},{8,7},{9,8},{10,9},{11,1... | collective-permute-start | bytes 3538952 | tf_op jit(solution)/shard_map/ppermute | solution.py:718
  100.7 16.2 %collective-permute-start.2 = (bf16[576,1024]{1,0:T(8,128)(2,1)}, bf16[576,1024]{1,0:T(8,128)(2,1)}, u32[]{:S(2)}, u32[]{:S(2)}) collective-permute-start(bf16[576,1024]{1,0:T(8,128)(2,1)} %get-tuple-element.85), channel_id=1, source_target_pairs={{0,1},{1,2},{2,3},{3,4},{4,5},{5,6},{6,7},{7,8},{8,9},{9,10},{10,1... | collective-permute-start | bytes 3538952 | tf_op jit(solution)/shard_map/ppermute | solution.py:717
  116.9 514.6 %reduce-scatter.2.cloned.1.call-start = ((), (), s32[]{:S(2)}) async-start(), calls=%async_computation.3 | async-start | bytes 19464192 | tf_op jit(solution)/shard_map/reduce_scatter | solution.py:655
  117.7 21.5 %collective-permute-start.1 = (s32[576]{0:T(1024)S(1)}, s32[576]{0:T(1024)S(1)}, u32[]{:S(2)}, u32[]{:S(2)}) collective-permute-start(s32[576]{0:T(1024)S(1)} %get-tuple-element.126), channel_id=1, source_target_pairs={{1,0},{2,1},{3,2},{4,3},{5,4},{6,5},{7,6},{8,7},{9,8},{10,9},{11,1... | collective-permute-start | bytes 6920 | tf_op jit(solution)/shard_map/ppermute | solution.py:721
  119.0 20.2 %collective-permute-start = (s32[576]{0:T(1024)S(1)}, s32[576]{0:T(1024)S(1)}, u32[]{:S(2)}, u32[]{:S(2)}) collective-permute-start(s32[576]{0:T(1024)S(1)} %get-tuple-element.127), channel_id=1, source_target_pairs={{0,1},{1,2},{2,3},{3,4},{4,5},{5,6},{6,7},{7,8},{8,9},{9,10},{10,1... | collective-permute-start | bytes 6920 | tf_op jit(solution)/shard_map/ppermute | solution.py:720
  230.3 30.7 %copy-start.25 = (f32[1,1024]{1,0:T(1,128)S(1)}, f32[1,1024]{1,0:T(1,128)}, u32[]{:S(2)}) copy-start(f32[1,1024]{1,0:T(1,128)} %get-tuple-element.109) | copy-start | bytes 12292
  267.8 71.6 %copy-start.4 = (f32[1024,1024]{1,0:T(8,128)S(1)}, f32[1024,1024]{1,0:T(8,128)}, u32[]{:S(2)}) copy-start(f32[1024,1024]{1,0:T(8,128)} %copy-done.3) | copy-start | bytes 12582916
  444.5 43.0 %collective-permute-start.4 = (bf16[576,2048]{1,0:T(8,128)(2,1)}, bf16[576,2048]{1,0:T(8,128)(2,1)}, u32[]{:S(2)}, u32[]{:S(2)}) collective-permute-start(bf16[576,2048]{1,0:T(8,128)(2,1)} %get-tuple-element.76), channel_id=1, source_target_pairs={{0,1},{1,2},{2,3},{3,4},{4,5},{5,6},{6,7},{7,8},{8,9},{9,10},{10,1... | collective-permute-start | bytes 7077896 | tf_op jit(solution)/shard_map/ppermute | solution.py:779
  456.4 31.1 %collective-permute-start.5 = (bf16[576,2048]{1,0:T(8,128)(2,1)}, bf16[576,2048]{1,0:T(8,128)(2,1)}, u32[]{:S(2)}, u32[]{:S(2)}) collective-permute-start(bf16[576,2048]{1,0:T(8,128)(2,1)} %get-tuple-element.77), channel_id=1, source_target_pairs={{1,0},{2,1},{3,2},{4,3},{5,4},{6,5},{7,6},{8,7},{9,8},{10,9},{11,1... | collective-permute-start | bytes 7077896 | tf_op jit(solution)/shard_map/ppermute | solution.py:778
  481.9 92.0 %collective-permute-start.11 = (bf16[16,96,1024]{2,1,0:T(8,128)(2,1)}, bf16[16,96,1024]{2,1,0:T(8,128)(2,1)}, u32[]{:S(2)}, u32[]{:S(2)}) collective-permute-start(bf16[16,96,1024]{2,1,0:T(8,128)(2,1)} %get-tuple-element.57), channel_id=1, source_target_pairs={{0,1},{1,0},{2,3},{3,2},{4,5},{5,4},{6,7},{7,6},{8,9},{9,8},{10,11... | collective-permute-start | bytes 9437192 | tf_op jit(solution)/shard_map/ppermute | solution.py:564
  509.4 64.5 %copy-start.11 = (bf16[16,96,1024]{2,1,0:T(8,128)(2,1)S(1)}, bf16[16,96,1024]{2,1,0:T(8,128)(2,1)}, u32[]{:S(2)}) copy-start(bf16[16,96,1024]{2,1,0:T(8,128)(2,1)} %get-tuple-element.56) | copy-start | bytes 9437188
  513.2 36.6 %collective-permute-start.6 = (f32[13,1024]{1,0:T(8,128)S(1)}, f32[13,1024]{1,0:T(8,128)S(1)}, u32[]{:S(2)}, u32[]{:S(2)}) collective-permute-start(f32[13,1024]{1,0:T(8,128)S(1)} %concatenate.36), channel_id=1, source_target_pairs={{0,1},{1,0},{2,3},{3,2},{4,5},{5,4},{6,7},{7,6},{8,9},{9,8},{10,11... | collective-permute-start | bytes 159752 | tf_op jit(solution)/shard_map/ppermute | solution.py:809
  549.9 6.0 collective-permute-start.7
  556.0 4.3 collective-permute-start.8
  560.4 6.8 %collective-permute-start.9 = (f32[13,1024]{1,0:T(8,128)S(1)}, f32[13,1024]{1,0:T(8,128)S(1)}, u32[]{:S(2)}, u32[]{:S(2)}) collective-permute-start(f32[13,1024]{1,0:T(8,128)S(1)} %add_select_fusion.2), channel_id=1, source_target_pairs={{0,8},{1,9},{2,10},{3,11},{4,12},{5,13},{6,14},{7,15},{8,0},{9,1},... | collective-permute-start | bytes 159752 | tf_op jit(solution)/shard_map/ppermute | solution.py:809
  567.2 18.0 %collective-permute-start.10 = (f32[13,1024]{1,0:T(8,128)S(1)}, f32[13,1024]{1,0:T(8,128)S(1)}, u32[]{:S(2)}, u32[]{:S(2)}) collective-permute-start(f32[13,1024]{1,0:T(8,128)S(1)} %add_select_fusion.1), channel_id=1, source_target_pairs={{0,16},{1,17},{2,18},{3,19},{4,20},{5,21},{6,22},{7,23},{8,24},{9,... | collective-permute-start | bytes 159752 | tf_op jit(solution)/shard_map/ppermute | solution.py:809
  576.1 21.6 %collective-permute-start.14 = (bf16[2,4,48,1024]{3,2,1,0:T(8,128)(2,1)S(1)}, bf16[2,4,48,1024]{3,2,1,0:T(8,128)(2,1)S(1)}, u32[]{:S(2)}, u32[]{:S(2)}) collective-permute-start(bf16[2,4,48,1024]{3,2,1,0:T(8,128)(2,1)S(1)} %get-tuple-element.81), channel_id=1, source_target_pairs={{0,4},{1,5},{2,6},{3,7},{4,0},{5,1},{6,2},{7,3},{8,12},{9,13},{10,... | collective-permute-start | bytes 2359304 | tf_op jit(solution)/shard_map/ppermute | solution.py:564
  580.1 24.4 %collective-permute-start.12 = (bf16[2,4,48,1024]{3,2,1,0:T(8,128)(2,1)S(1)}, bf16[2,4,48,1024]{3,2,1,0:T(8,128)(2,1)S(1)}, u32[]{:S(2)}, u32[]{:S(2)}) collective-permute-start(bf16[2,4,48,1024]{3,2,1,0:T(8,128)(2,1)S(1)} %get-tuple-element.79), channel_id=1, source_target_pairs={{0,2},{1,3},{2,0},{3,1},{4,6},{5,7},{6,4},{7,5},{8,10},{9,11},{10,... | collective-permute-start | bytes 2359304 | tf_op jit(solution)/shard_map/ppermute | solution.py:564
  598.0 11.5 %collective-permute-start.15 = (bf16[4,48,1024]{2,1,0:T(8,128)(2,1)S(1)}, bf16[4,48,1024]{2,1,0:T(8,128)(2,1)S(1)}, u32[]{:S(2)}, u32[]{:S(2)}) collective-permute-start(bf16[4,48,1024]{2,1,0:T(8,128)(2,1)S(1)} %get-tuple-element.89), channel_id=1, source_target_pairs={{0,2},{1,3},{2,0},{3,1},{4,6},{5,7},{6,4},{7,5},{8,10},{9,11},{10,... | collective-permute-start | bytes 1179656 | tf_op jit(solution)/shard_map/ppermute | solution.py:564
  604.9 7.8 %collective-permute-start.13 = (bf16[4,48,1024]{2,1,0:T(8,128)(2,1)S(1)}, bf16[4,48,1024]{2,1,0:T(8,128)(2,1)S(1)}, u32[]{:S(2)}, u32[]{:S(2)}) collective-permute-start(bf16[4,48,1024]{2,1,0:T(8,128)(2,1)S(1)} %get-tuple-element.87), channel_id=1, source_target_pairs={{0,4},{1,5},{2,6},{3,7},{4,0},{5,1},{6,2},{7,3},{8,12},{9,13},{10,... | collective-permute-start | bytes 1179656 | tf_op jit(solution)/shard_map/ppermute | solution.py:564
  612.9 9.9 %collective-permute-start.16 = (bf16[2,96,1024]{2,1,0:T(8,128)(2,1)S(1)}, bf16[2,96,1024]{2,1,0:T(8,128)(2,1)S(1)}, u32[]{:S(2)}, u32[]{:S(2)}) collective-permute-start(bf16[2,96,1024]{2,1,0:T(8,128)(2,1)S(1)} %pad_maximum_fusion.2), channel_id=1, source_target_pairs={{0,8},{1,9},{2,10},{3,11},{4,12},{5,13},{6,14},{7,15},{8,0},{9,1},... | collective-permute-start | bytes 1179656 | tf_op jit(solution)/shard_map/ppermute | solution.py:564
  622.9 7.9 %collective-permute-start.17 = (bf16[96,1024]{1,0:T(8,128)(2,1)S(1)}, bf16[96,1024]{1,0:T(8,128)(2,1)S(1)}, u32[]{:S(2)}, u32[]{:S(2)}) collective-permute-start(bf16[96,1024]{1,0:T(8,128)(2,1)S(1)} %fusion.14), channel_id=1, source_target_pairs={{0,16},{1,17},{2,18},{3,19},{4,20},{5,21},{6,22},{7,23},{8,24},{9,... | collective-permute-start | bytes 589832 | tf_op jit(solution)/shard_map/ppermute | solution.py:564
  (25 other events, 341.7 us)
Sparse Core Ops, SparseCore 0:
  18.8 74.1 all-gather.2
  117.1 140.0 all-gather.4
  357.9 246.2 reduce-scatter.1

commit v2 on v1

--- a/solution.py
+++ b/solution.py
@@ -11,7 +11,7 @@
 HD = 64
 LEN = 577
 RIM = LEN - 1
-PAIR = 2 * HD
+HEADS = 4
 QB = 256
 KB = 256
 
@@ -51,12 +51,34 @@
     return jnp.sum(values.astype(f32), axis=0)
 
 
-def two_heads(block):
-    lane = lax.broadcasted_iota(jnp.int32, block.shape, 1)
+def cost(flops):
+    return pl.CostEstimate(flops=flops, transcendentals=0, bytes_accessed=flops // 500)
+
+
+def by_head(block):
+    lane = lax.broadcasted_iota(jnp.int32, block.shape, 1) // HD
     zero = jnp.zeros_like(block)
-    return jnp.concatenate(
-        [jnp.where(lane < HD, block, zero), jnp.where(lane >= HD, block, zero)], axis=0
-    )
+    return jnp.concatenate([jnp.where(lane == i, block, zero) for i in range(HEADS)], axis=0)
+
+
+def pair_slices(p):
+    return slice(p * 2 * HD, (p + 1) * 2 * HD), slice(p * 2 * QB, (p + 1) * 2 * QB)
+
+
+def untangle(parts):
+    joined = []
+    for part in parts:
+        joined.append(jnp.concatenate([part[:HD, :QB], part[HD:, QB:]], axis=0).T)
+    return jnp.concatenate(joined, axis=1)
+
+
+def by_twos(count, step, start):
+    two = lambda i, carry: step(2 * i + 1, step(2 * i, carry))
+    return lax.fori_loop(count // 2 * 2, count, step, lax.fori_loop(0, count // 2, two, start))
+
+
+def widen(bias):
+    return jnp.concatenate([bias] * HEADS, axis=1)
 
 
 def fill_bias(bias_ref, key_ids_ref, query_ids_ref, block, low, count):
@@ -71,41 +93,55 @@
 
 
 def attend_kernel(
-    low_ref, count_ref, key_ids_ref, query_ids_ref, q_ref, k_ref, v_ref, o_ref, wide_ref, lse_ref, top_ref, bias_ref
+    low_ref, count_ref, key_ids_ref, query_ids_ref, q_ref, k_ref, v_ref,
+    o_ref, wide_ref, lse_ref, top_ref, bias_ref, score_ref,
 ):
-    pair, block = pl.program_id(0), pl.program_id(1)
+    group, block = pl.program_id(0), pl.program_id(1)
     low, count = low_ref[block], count_ref[block]
 
-    @pl.when(pair == 0)
+    @pl.when(group == 0)
     def _():
         fill_bias(bias_ref, key_ids_ref, query_ids_ref, block, low, count)
 
-    queries = two_heads(q_ref[...])
+    queries = by_head(q_ref[...] * jnp.asarray(SCALE, bf16))
     width = queries.shape[0]
-
-    def step(c, carry):
-        top, total, acc = carry
+    pairs = HEADS // 2
+
+    def score(c):
         start = pl.multiple_of(low + c * KB, 128)
-        bias = bias_ref[block, pl.ds(pl.multiple_of(c * KB, KB), KB), :]
-        scores = dot(k_ref[pl.ds(start, KB), :], queries, NT) * SCALE
-        scores = scores + jnp.concatenate([bias, bias], axis=1)
-        new_top = jnp.maximum(top, jnp.max(scores, axis=0, keepdims=True))
-        weights = jnp.exp(scores - new_top)
-        fade = jnp.exp(top - new_top)
-        total = total * fade + jnp.sum(weights, axis=0, keepdims=True)
-        acc = acc * fade + dot(v_ref[pl.ds(start, KB), :], weights.astype(bf16), TN)
-        return new_top, total, acc
-
-    start_top = jnp.full((1, width), NEG_FILL, f32)
-    top, total, acc = lax.fori_loop(
-        0, count, step, (start_top, jnp.zeros((1, width), f32), jnp.zeros((PAIR, width), f32))
-    )
-    mixed = acc / total
-    half = width // 2
-    joined = jnp.concatenate([mixed[:HD, :half], mixed[HD:, half:]], axis=0)
-    joined = joined.T
-    wide_ref[...] = joined
-    o_ref[...] = joined.astype(bf16)
+        return dot(k_ref[pl.ds(start, KB), :], queries, NT)
+
+    def fold(op, tile):
+        return op(tile.reshape(KB // 8, 8, width), axis=0)
+
+    def first(c, top):
+        at = pl.ds(pl.multiple_of(c * KB, KB), KB)
+        scores = score(c) + widen(bias_ref[block, at, :])
+        score_ref[at, :] = scores
+        return jnp.maximum(top, fold(jnp.max, scores))
+
+    top = by_twos(count, first, jnp.full((8, width), NEG_FILL, f32))
+    top = jnp.max(top, axis=0, keepdims=True)
+
+    def second(c, carry):
+        total, accs = carry
+        start = pl.multiple_of(low + c * KB, 128)
+        weights = jnp.exp(score_ref[pl.ds(pl.multiple_of(c * KB, KB), KB), :] - top)
+        total = total + fold(jnp.sum, weights)
+        low_weights = weights.astype(bf16)
+        values = v_ref[pl.ds(start, KB), :]
+        new_accs = []
+        for p, acc in enumerate(accs):
+            lanes, place = pair_slices(p)
+            new_accs.append(acc + dot(values[:, lanes], low_weights[:, place], TN))
+        return total, tuple(new_accs)
+
+    zeros = tuple(jnp.zeros((2 * HD, 2 * QB), f32) for _ in range(pairs))
+    total, accs = by_twos(count, second, (jnp.zeros((8, width), f32), zeros))
+    total = jnp.sum(total, axis=0, keepdims=True)
+    mixed = untangle([acc / total[:, pair_slices(p)[1]] for p, acc in enumerate(accs)])
+    wide_ref[...] = mixed
+    o_ref[...] = mixed.astype(bf16)
     lse_ref[0] = top + jnp.log(total)
 
     @pl.when(block == 0)
@@ -147,39 +183,37 @@
         dk_acc[...] = jnp.zeros_like(dk_acc)
         dv_acc[...] = jnp.zeros_like(dv_acc)
 
-    queries = two_heads(q_ref[...])
-    grads = two_heads(do_ref[...])
-    mixed = jnp.concatenate([o_ref[...], o_ref[...]], axis=0)
-    inner = lax.dot_general(
-        jnp.ones((8, PAIR), f32),
-        grads.astype(f32) * mixed,
-        NT,
-        precision=lax.Precision.HIGHEST,
-        preferred_element_type=f32,
-    )[0:1]
+    queries = by_head(q_ref[...] * jnp.asarray(SCALE, bf16))
+    grads = by_head(do_ref[...])
+    product = (do_ref[...].astype(f32) * o_ref[...]).T
+    inner = jnp.concatenate(
+        [jnp.sum(product[i * HD : (i + 1) * HD], axis=0, keepdims=True) for i in range(HEADS)], axis=1
+    )
     log_sum = lse_ref[0]
-    width = queries.shape[0]
-
-    def step(c, acc):
+    pairs = HEADS // 2
+
+    def step(c, accs):
         start = pl.multiple_of(low + c * KB, 128)
         keys = k_ref[pl.ds(start, KB), :]
         bias = bias_ref[block, pl.ds(pl.multiple_of(c * KB, KB), KB), :]
-        scores = dot(keys, queries, NT) * SCALE + jnp.concatenate([bias, bias], axis=1)
+        scores = dot(keys, queries, NT) + widen(bias)
         probs = jnp.exp(scores - log_sum)
         prob_grad = dot(v_ref[pl.ds(start, KB), :], grads, NT)
         score_grad = (probs * (prob_grad - inner)).astype(bf16)
         dv_acc[pl.ds(start, KB), :] += dot(probs.astype(bf16), grads, NN)
         dk_acc[pl.ds(start, KB), :] += dot(score_grad, queries, NN)
-        return acc + dot(keys, score_grad, TN)
-
-    acc = lax.fori_loop(0, count, step, jnp.zeros((PAIR, width), f32))
-    half = width // 2
-    joined = jnp.concatenate([acc[:HD, :half], acc[HD:, half:]], axis=0) * SCALE
-    dq_ref[...] = joined.T.astype(bf16)
+        new_accs = []
+        for p, acc in enumerate(accs):
+            lanes, place = pair_slices(p)
+            new_accs.append(acc + dot(keys[:, lanes], score_grad[:, place], TN))
+        return tuple(new_accs)
+
+    zeros = tuple(jnp.zeros((2 * HD, 2 * QB), f32) for _ in range(pairs))
+    dq_ref[...] = (untangle(by_twos(count, step, zeros)) * SCALE).astype(bf16)
 
     @pl.when(block == pl.num_programs(1) - 1)
     def _():
-        dk_ref[...] = (dk_acc[...] * SCALE).astype(bf16)
+        dk_ref[...] = dk_acc[...].astype(bf16)
         dv_ref[...] = dv_acc[...].astype(bf16)
 
 
@@ -198,43 +232,45 @@
 
 
 def attention_specs(rows, near, blocks):
-    pairs = H // 2
+    groups = H // HEADS
+    span = HEADS * HD
     most = -(-(QB + 2 * RIM + 127) // KB) * KB
     assert most <= near and rows % QB == 0 and near % 128 == 0
-    own = pl.BlockSpec((QB, PAIR), lambda p, b, *_: (b, p))
+    own = pl.BlockSpec((QB, span), lambda p, b, *_: (b, p))
     base = [
         pl.BlockSpec((near, 1), lambda p, b, *_: (0, 0)),
         pl.BlockSpec((1, QB), lambda p, b, *_: (0, b)),
         own,
-        pl.BlockSpec((near, PAIR), lambda p, b, *_: (0, p)),
-        pl.BlockSpec((near, PAIR), lambda p, b, *_: (0, p + pairs)),
+        pl.BlockSpec((near, span), lambda p, b, *_: (0, p)),
+        pl.BlockSpec((near, span), lambda p, b, *_: (0, p + groups)),
     ]
-    row = pl.BlockSpec((1, 1, 2 * QB), lambda p, b, *_: (p, 0, b))
+    row = pl.BlockSpec((1, 1, HEADS * QB), lambda p, b, *_: (p, 0, b))
     bias = pltpu.VMEM((blocks, most, QB), f32)
-    return pairs, own, base, row, bias
+    return groups, own, base, row, bias
 
 
 def attend(ranges, key_ids, query_ids, queries, near_kv):
     rows, near = queries.shape[0], near_kv.shape[0]
     blocks = rows // QB
-    pairs, own, base, row, bias = attention_specs(rows, near, blocks)
-    top = pl.BlockSpec((1, 1, 2 * QB), lambda p, b, *_: (p, 0, 0))
+    groups, own, base, row, bias = attention_specs(rows, near, blocks)
+    top = pl.BlockSpec((1, 1, HEADS * QB), lambda p, b, *_: (p, 0, 0))
     return pl.pallas_call(
         attend_kernel,
         grid_spec=pltpu.PrefetchScalarGridSpec(
             num_scalar_prefetch=2,
-            grid=(pairs, blocks),
+            grid=(groups, blocks),
             in_specs=base,
             out_specs=[own, own, row, top],
-            scratch_shapes=[bias],
+            scratch_shapes=[bias, pltpu.VMEM((bias.shape[1], HEADS * QB), f32)],
         ),
         out_shape=[
             jax.ShapeDtypeStruct(queries.shape, bf16),
             jax.ShapeDtypeStruct(queries.shape, f32),
-            jax.ShapeDtypeStruct((pairs, 1, 2 * rows), f32),
-            jax.ShapeDtypeStruct((pairs, 1, 2 * QB), f32),
+            jax.ShapeDtypeStruct((groups, 1, HEADS * rows), f32),
+            jax.ShapeDtypeStruct((groups, 1, HEADS * QB), f32),
         ],
         compiler_params=pltpu.CompilerParams(vmem_limit_bytes=56 << 20),
+        cost_estimate=cost(rows * H * HD * 850 * 16),
         name="attend",
     )(*ranges, key_ids, query_ids, queries, near_kv, near_kv)
 
@@ -242,16 +278,16 @@
 def attend_back(ranges, key_ids, query_ids, queries, near_kv, mixed_grad, mixed, log_sums):
     rows, near = queries.shape[0], near_kv.shape[0]
     blocks = rows // QB
-    pairs, own, base, row, bias = attention_specs(rows, near, blocks)
-    wide = pl.BlockSpec((near, PAIR), lambda p, b, *_: (0, p))
+    groups, own, base, row, bias = attention_specs(rows, near, blocks)
+    wide = pl.BlockSpec((near, HEADS * HD), lambda p, b, *_: (0, p))
     return pl.pallas_call(
         attend_back_kernel,
         grid_spec=pltpu.PrefetchScalarGridSpec(
             num_scalar_prefetch=2,
-            grid=(pairs, blocks),
+            grid=(groups, blocks),
             in_specs=base + [own, own, row],
             out_specs=[own, wide, wide],
-            scratch_shapes=[bias, pltpu.VMEM((near, PAIR), f32), pltpu.VMEM((near, PAIR), f32)],
+            scratch_shapes=[bias, pltpu.VMEM((near, HEADS * HD), f32), pltpu.VMEM((near, HEADS * HD), f32)],
         ),
         out_shape=[
             jax.ShapeDtypeStruct(queries.shape, bf16),
@@ -259,8 +295,17 @@
             jax.ShapeDtypeStruct((near, queries.shape[1]), bf16),
         ],
         compiler_params=pltpu.CompilerParams(vmem_limit_bytes=56 << 20),
+        cost_estimate=cost(rows * H * HD * 850 * 32),
         name="attend_back",
     )(*ranges, key_ids, query_ids, queries, near_kv, near_kv, mixed_grad, mixed, log_sums)
+
+
+def spot_of(place, half):
+    spot, bit = 0, half
+    while bit:
+        spot = spot + (place & 1) * bit
+        place, bit = place >> 1, bit >> 1
+    return spot
 
 
 def mlp_kernel(
@@ -371,60 +416,71 @@
             pltpu.SemaphoreType.DMA((2,)),
         ],
         compiler_params=pltpu.CompilerParams(vmem_limit_bytes=58 << 20),
+        cost_estimate=cost(12 * rows * width * ff),
         name="mlp",
     )(normed, branch_grad, middle, bias_reduce, bias_expand, packed, packed)
 
 
-def out_back_kernel(ag_ref, mixed_ref, wo_ref, sum_in_ref, mg_ref, sum_ref, og_ref, sem):
+def out_back_kernel(me_ref, ag_ref, mixed_ref, wo_ref, mg_ref, keep_ref, send_ref):
     rows, width = ag_ref.shape
     tile = 256
-    groups, each, _ = og_ref.shape
+    half, each, _ = keep_ref.shape
 
     def by_columns(t, carry):
         at = pl.ds(pl.multiple_of(t * tile, tile), tile)
         og = dot(mixed_ref[:, at], ag_ref[...], TN).astype(bf16)
         n = tile // each
-        og_ref[pl.ds(t * n, n)] = og.reshape(n, each, width)
+        for i in range(n):
+            spot = spot_of((t * n + i) ^ me_ref[0], half)
+            block = og[i * each : (i + 1) * each]
+
+            @pl.when(spot < half)
+            def _():
+                keep_ref[spot] = block
+
+            @pl.when(spot >= half)
+            def _():
+                send_ref[spot - half] = block
+
         return carry
 
     lax.fori_loop(0, width // tile, by_columns, 0)
-    copy = pltpu.make_async_copy(og_ref, sum_ref.at[:, pl.ds(sum_ref.shape[1] - each, each), :], sem)
-    copy.start()
-
     def by_rows(t, carry):
         at = pl.ds(pl.multiple_of(t * tile, tile), tile)
         mg_ref[at, :] = dot(ag_ref[at, :], wo_ref[...].reshape(width, width), NT).astype(bf16)
         return carry
 
     lax.fori_loop(0, rows // tile, by_rows, 0)
-    copy.wait()
-
-
-def out_back(attn_grad, mixed, packed, sums):
+
+
+def out_back(attn_grad, mixed, packed, last, place):
     rows, width = attn_grad.shape
     groups = packed.shape[0]
     each = width // groups
-    last = sums.shape[1] // each - 1
-    whole = lambda i: (0, 0)
+    whole = lambda i, *_: (0, 0)
+    side = pl.BlockSpec((groups // 2, each, width), lambda i, *_: (0, 0, 0))
+    half = jax.ShapeDtypeStruct((groups // 2, each, width), bf16)
     return pl.pallas_call(
         out_back_kernel,
-        grid=(1,),
-        in_specs=[
-            pl.BlockSpec((rows, width), whole),
-            pl.BlockSpec((rows, width), whole),
-            pl.BlockSpec((groups, each, width), lambda i: (0, last, 0)),
-            pl.BlockSpec(memory_space=pl.ANY),
-        ],
-        out_specs=[pl.BlockSpec((rows, width), whole), pl.BlockSpec(memory_space=pl.ANY)],
+        grid_spec=pltpu.PrefetchScalarGridSpec(
+            num_scalar_prefetch=1,
+            grid=(1,),
+            in_specs=[
+                pl.BlockSpec((rows, width), whole),
+                pl.BlockSpec((rows, width), whole),
+                pl.BlockSpec((groups, each, width), lambda i, *_: (0, last, 0)),
+            ],
+            out_specs=[pl.BlockSpec((rows, width), whole), side, side],
+        ),
         out_shape=[
             jax.ShapeDtypeStruct((rows, width), bf16),
-            jax.ShapeDtypeStruct(sums.shape, bf16),
-        ],
-        scratch_shapes=[pltpu.VMEM((groups, each, width), bf16), pltpu.SemaphoreType.DMA(())],
-        input_output_aliases={3: 1},
+            half,
+            half,
+        ],
         compiler_params=pltpu.CompilerParams(vmem_limit_bytes=56 << 20),
+        cost_estimate=cost(4 * rows * width * width),
         name="out_back",
-    )(attn_grad, mixed, packed, sums)
+    )(place, attn_grad, mixed, packed)
 
 
 def qkv_kernel(a_ref, w_ref, bias_ref, q_ref, kv_ref):
@@ -479,6 +535,7 @@
             jax.ShapeDtypeStruct((near, 2 * width), bf16),
         ],
         compiler_params=pltpu.CompilerParams(vmem_limit_bytes=56 << 20),
+        cost_estimate=cost(2 * width * width * (rows + 2 * near)),
         name="qkv",
     )(normed_near, packed, biases)
 
@@ -497,11 +554,7 @@
             at = pl.ds(pl.multiple_of(t * tile, tile), tile)
             out = dot(a_ref[source, at], grad_ref[...], TN).astype(bf16)
             for i in range(n):
-                place = (t * n + i) ^ me_ref[0]
-                spot, bit = 0, half
-                while bit:
-                    spot = spot + (place & 1) * bit
-                    place, bit = place >> 1, bit >> 1
+                spot = spot_of((t * n + i) ^ me_ref[0], half)
                 block = out[i * each : (i + 1) * each]
 
                 @pl.when(spot < half)
@@ -551,8 +604,9 @@
         ),
         out_shape=[half, half],
         compiler_params=pltpu.CompilerParams(vmem_limit_bytes=56 << 20),
+        cost_estimate=cost(2 * width * width * (rows + 2 * near)),
         name="qkv_grads",
-    )(jnp.full((1,), place, jnp.int32), normed_near, query_grad, key_near, value_near)
+    )(place, normed_near, query_grad, key_near, value_near)
 
 
 def plus(a, b):
@@ -564,65 +618,162 @@
     return lax.ppermute(value, "dev", [(i, i ^ bit) for i in range(peers)])
 
 
-def halving(keep, send):
-    _, rows, width = keep.shape
-    half = rows // 2
-    other = swap(send, 1).reshape(2, 2, 4, rows, width)
-    keep = keep.reshape(2, 2, 4, rows, width)
-    a, b = slice(0, half), slice(half, rows)
-    from_x = swap(plus(keep[1, :, :, a], other[1, :, :, a]), 2)
-    from_y = swap(plus(keep[:, 1, :, b], other[:, 1, :, b]), 4)
-    keep_x = plus(keep[0, :, :, a], other[0, :, :, a])
-    keep_y = plus(keep[:, 0, :, b], other[:, 0, :, b])
-    second_y = swap(plus(keep_x[1], from_x[1]), 4)
-    second_x = swap(plus(keep_y[1], from_y[1]), 2)
+def merge(totals, bit):
+    other = swap(totals, bit)
+    return jnp.concatenate([totals[:-1] + other[:-1], jnp.maximum(totals[-1:], other[-1:])], axis=0)
+
+
+def halving(first, second, totals):
+    def split(pair):
+        keep, other = (v.reshape((2, 2, 4) + v.shape[1:]) for v in pair)
+        return keep, other
+
+    (keep, other), (keep_o, other_o) = split(first), split(second)
+    half = (keep.shape[3] + keep_o.shape[3]) // 2
+
+    def side_a(at):
+        return plus(keep[at][..., :half, :], other[at][..., :half, :])
+
+    def side_b(at):
+        return jnp.concatenate(
+            [plus(keep[at][..., half:, :], other[at][..., half:, :]), plus(keep_o[at], other_o[at])], axis=-2
+        )
+
+    to_x, to_y = side_a(1), side_b((slice(None), 1))
+    to_x, to_y, totals = lax.optimization_barrier((to_x, to_y, totals))
+    from_x, from_y = swap(to_x, 2), swap(to_y, 4)
+    totals = merge(totals, 1)
+    keep_x, keep_y = side_a(0), side_b((slice(None), 0))
+    to_y, to_x = plus(keep_x[1], from_x[1]), plus(keep_y[1], from_y[1])
+    to_x, to_y, totals = lax.optimization_barrier((to_x, to_y, totals))
+    second_y, second_x = swap(to_y, 4), swap(to_x, 2)
+    totals = merge(totals, 2)
     keep_x = plus(keep_x[0], from_x[0])
     keep_y = plus(keep_y[0], from_y[0])
     send = jnp.concatenate([plus(keep_x[2:], second_y[2:]), plus(keep_y[2:], second_x[2:])], axis=1)
+    send, totals = lax.optimization_barrier((send, totals))
     low = swap(send, 8)
+    totals = merge(totals, 4)
     keep = jnp.concatenate([plus(keep_x[:2], second_y[:2]), plus(keep_y[:2], second_x[:2])], axis=1)
-    last = swap(plus(keep[1], low[1]), 16)
-    return plus(keep[0], low[0]).astype(f32) + last.astype(f32)
-
-
-def normed_grad_kernel(dq_ref, dkv_ref, w_ref, out_ref):
+    send, totals = lax.optimization_barrier((plus(keep[1], low[1]), totals))
+    last = swap(send, 16)
+    totals = merge(merge(totals, 8), 16)
+    return plus(keep[0], low[0]).astype(f32) + last.astype(f32), totals
+
+
+def plain(pairs, part):
+    groups = 2 * pairs[0][0].shape[0]
+    order = [int(f"{i:05b}"[::-1], 2) for i in range(groups)]
+    joined = jnp.concatenate([jnp.concatenate(pair, axis=0) for pair in pairs], axis=1)
+    joined = jnp.stack([joined[i] for i in order])
+    return scatter(joined, [part] * (joined.shape[1] * groups // joined.shape[2])).astype(f32)
+
+
+def normed_grad_kernel(
+    dq_ref, dk_ref, dv_ref, w_ref, normal_ref, nb_ref, na_ref,
+    own_ref, before_ref, after_ref, sums_ref, acc_b, acc_a,
+):
     j = pl.program_id(0)
-    rows, width = out_ref.shape
-
-    def step(t, carry):
-        at = pl.ds(pl.multiple_of(t * 256, 256), 256)
-        w = w_ref[...].reshape(width, width)
-
-        @pl.when(j == 0)
-        def _():
-            out_ref[at, :] = dot(dq_ref[at, :], w, NT)
-
-        @pl.when(j > 0)
-        def _():
-            out_ref[at, :] += dot(dkv_ref[at, :], w, NT)
-
-        return carry
-
-    lax.fori_loop(0, rows // 256, step, 0)
-
-
-def project_back(query_grad, kv_grad, packed):
+    rows, width = own_ref.shape
+    rim = before_ref.shape[0]
+
+    def by_rows(total, size, act):
+        def step(t, carry):
+            act(pl.multiple_of(t * size, size))
+            return carry
+
+        lax.fori_loop(0, total // size, step, 0)
+
+    def near(grad_ref, first):
+        def add(out_ref, base, size):
+            def act(at):
+                w = w_ref[...].reshape(width, width)
+                part = dot(grad_ref[pl.ds(pl.multiple_of(base + at, 8), size), :], w, NT)
+                spot = pl.ds(at, size)
+                out_ref[spot, :] = part if first else out_ref[spot, :] + part
+
+            return act
+
+        by_rows(rim, rim // 2, add(acc_b, 0, rim // 2))
+        by_rows(rim, rim // 2, add(acc_a, rim + rows, rim // 2))
+
+        def act(at):
+            w = w_ref[...].reshape(width, width)
+            own_ref[pl.ds(at, 256), :] += dot(grad_ref[pl.ds(pl.multiple_of(rim + at, 8), 256), :], w, NT)
+
+        by_rows(rows, 256, act)
+
+    @pl.when(j == 0)
+    def _():
+        sums_ref[...] = jnp.zeros_like(sums_ref)
+
+        def act(at):
+            spot = pl.ds(at, 256)
+            w = w_ref[...].reshape(width, width)
+            grads = dq_ref[spot, :]
+            own_ref[spot, :] = dot(grads, w, NT)
+
+        by_rows(rows, 256, act)
+
+    @pl.when(j == 1)
+    def _():
+        near(dk_ref, True)
+
+    @pl.when(j == 2)
+    def _():
+        near(dv_ref, False)
+
+        def finish(source, normal, out, carry):
+            def step(t, carry):
+                gain_sum, bias_sum = carry
+                spot = pl.ds(pl.multiple_of(t * 16, 16), 16)
+                value = source[spot, :]
+                product = value * normal[spot, :].astype(f32)
+                if out is not None:
+                    out[spot, :] = value.astype(bf16)
+                return gain_sum + product[:8] + product[8:], bias_sum + value[:8] + value[8:]
+
+            return lax.fori_loop(0, source.shape[0] // 16, step, carry)
+
+        carry = (jnp.zeros((8, width), f32), jnp.zeros((8, width), f32))
+        carry = finish(acc_b, nb_ref, before_ref, carry)
+        carry = finish(acc_a, na_ref, after_ref, carry)
+        gain_sum, bias_sum = finish(own_ref, normal_ref, None, carry)
+        sums_ref[0:1, :] = jnp.sum(gain_sum, axis=0, keepdims=True)
+        sums_ref[1:2, :] = jnp.sum(bias_sum, axis=0, keepdims=True)
+        sums_ref[2:3, :] = dot(jnp.ones((8, rows), bf16), dq_ref[...], NN)[0:1]
+        sums_ref[3:4, :] = dot(jnp.ones((8, 2 * rim + rows), bf16), dv_ref[...], NN)[0:1]
+
+
+def project_back(query_grad, key_near, value_near, packed, normal, before, after):
     rows, width = query_grad.shape
+    near, rim = key_near.shape[0], before.shape[0]
     groups = packed.shape[0]
     each = width // groups
+    whole = lambda j: (0, 0)
+    one = pl.Buffered(1)
+    own, wide, side = (pl.BlockSpec((n, width), whole, pipeline_mode=one) for n in (rows, near, rim))
     return pl.pallas_call(
         normed_grad_kernel,
         grid=(3,),
-        in_specs=[
-            pl.BlockSpec((rows, width), lambda j: (0, 0)),
-            pl.BlockSpec((rows, width), lambda j: (0, jnp.maximum(j - 1, 0))),
-            pl.BlockSpec((groups, each, width), lambda j: (0, j, 0)),
-        ],
-        out_specs=pl.BlockSpec((rows, width), lambda j: (0, 0)),
-        out_shape=jax.ShapeDtypeStruct((rows, width), f32),
-        compiler_params=pltpu.CompilerParams(vmem_limit_bytes=56 << 20),
+        in_specs=[own, wide, wide, pl.BlockSpec((groups, each, width), lambda j: (0, j, 0)), own, side, side],
+        out_specs=[
+            pl.BlockSpec((rows, width), whole),
+            pl.BlockSpec((rim, width), whole),
+            pl.BlockSpec((rim, width), whole),
+            pl.BlockSpec((4, width), whole),
+        ],
+        out_shape=[
+            jax.ShapeDtypeStruct((rows, width), f32),
+            jax.ShapeDtypeStruct((rim, width), bf16),
+            jax.ShapeDtypeStruct((rim, width), bf16),
+            jax.ShapeDtypeStruct((4, width), f32),
+        ],
+        scratch_shapes=[pltpu.VMEM((rim, width), f32), pltpu.VMEM((rim, width), f32)],
+        compiler_params=pltpu.CompilerParams(vmem_limit_bytes=58 << 20),
+        cost_estimate=cost(2 * width * width * (rows + 2 * near)),
         name="normed_grad",
-    )(query_grad, kv_grad, packed)
+    )(query_grad, key_near, value_near, packed, normal, before, after)
 
 
 def gather(value, segments, groups):
@@ -653,6 +804,95 @@
         value = jnp.concatenate(parts, axis=2)
     value = value.reshape(peers * sum(segments), width)
     return lax.psum_scatter(value, "dev", scatter_dimension=0, tiled=True)
+
+
+def pack_kernel(me_ref, q_ref, k_ref, v_ref, small_ref, r_ref, e_ref, o_ref, eb_ref, one_ref, two_ref):
+    part, width = q_ref.shape
+    for i, ref in enumerate((q_ref, k_ref, v_ref)):
+        one_ref[i * part : (i + 1) * part, :] = ref[...].astype(bf16)
+
+    def place(value, size):
+        index = lax.broadcasted_iota(jnp.int32, value.shape, 0) * width
+        index = index + lax.broadcasted_iota(jnp.int32, value.shape, 1)
+        return jnp.where(index // size == me_ref[0], value, jnp.zeros_like(value))
+
+    lane = lax.broadcasted_iota(jnp.int32, (8, width), 1)
+    one_ref[3 * part :, :] = jnp.where(lane // part == me_ref[0], small_ref[...], 0.0).astype(bf16)
+    rows = r_ref.shape[0]
+    fold = rows // part
+    two_ref[:rows, :] = r_ref[...].astype(bf16)
+    for i in range(fold):
+        at = rows + i * part
+        two_ref[at : at + part, :] = e_ref[:, i * width : (i + 1) * width].astype(bf16)
+    at = rows + fold * part
+    two_ref[at : at + part, :] = o_ref[...].astype(bf16)
+    two_ref[at + part :, :] = place(jnp.broadcast_to(eb_ref[...], (8, width)), fold * part).astype(bf16)
+
+
+def pack(me, mats, smalls, reduce_mat, expand_mat, output_mat, expand_bias):
+    part, width = output_mat.shape
+    tiled = jnp.stack([jnp.tile(v, width // part) for v in smalls])
+    bias = jnp.tile(expand_bias, width // expand_bias.shape[0])[None]
+    rows = reduce_mat.shape[0]
+    return pl.pallas_call(
+        pack_kernel,
+        grid_spec=pltpu.PrefetchScalarGridSpec(
+            num_scalar_prefetch=1,
+            grid=(1,),
+            in_specs=[
+                pl.BlockSpec(v.shape, lambda i, *_: (0, 0))
+                for v in (*mats, tiled, reduce_mat, expand_mat, output_mat, bias)
+            ],
+            out_specs=[
+                pl.BlockSpec((3 * part + 8, width), lambda i, *_: (0, 0)),
+                pl.BlockSpec((2 * rows + part + 8, width), lambda i, *_: (0, 0)),
+            ],
+        ),
+        out_shape=[
+            jax.ShapeDtypeStruct((3 * part + 8, width), bf16),
+            jax.ShapeDtypeStruct((2 * rows + part + 8, width), bf16),
+        ],
+        name="pack",
+    )(jnp.full((1,), me, jnp.int32), *mats, tiled, reduce_mat, expand_mat, output_mat, bias)
+
+
+def place_kernel(me_ref, a_ref, ac_ref, b_ref, bc_ref, out_ref):
+    half = out_ref.shape[2] // 2
+    for core, (left, right) in enumerate(((a_ref, b_ref), (ac_ref, bc_ref))):
+        for spot in range(16):
+            high, low, z8, z16 = spot >> 3 & 1, spot >> 2 & 1, spot >> 1 & 1, spot & 1
+            z = z8 * 8 + z16 * 16 + core
+            out_ref[(z + high * 4 + low * 2) ^ me_ref[0], :, :half] = left[spot]
+            out_ref[(z + high * 2 + low * 4) ^ me_ref[0], :, half:] = right[spot]
+
+
+def doubling(value, me, beside):
+    rows, width = value.shape
+    half = width // 2
+    grown = value[None]
+    grown = jnp.concatenate([grown, swap(grown, 16)])
+    other = swap(grown, 8)
+    grown, other, *beside = lax.optimization_barrier((grown, other, *beside))
+    a = jnp.concatenate([grown[..., :half], other[..., :half]])
+    b = jnp.concatenate([grown[..., half:], other[..., half:]])
+    from_x, from_y = swap(a, 2), swap(b, 4)
+    a, b = jnp.concatenate([a, from_x]), jnp.concatenate([b, from_y])
+    from_y, from_x = swap(a, 4), swap(b, 2)
+    a, b = jnp.concatenate([a, from_y]), jnp.concatenate([b, from_x])
+    block = pl.BlockSpec(a.shape, lambda i, *_: (0, 0, 0))
+    placed = pl.pallas_call(
+        place_kernel,
+        grid_spec=pltpu.PrefetchScalarGridSpec(
+            num_scalar_prefetch=1,
+            grid=(1,),
+            in_specs=[block] * 4,
+            out_specs=pl.BlockSpec((32, rows, width), lambda i, *_: (0, 0, 0)),
+        ),
+        out_shape=jax.ShapeDtypeStruct((32, rows, width), bf16),
+        compiler_params=pltpu.CompilerParams(vmem_limit_bytes=56 << 20),
+        name="place",
+    )(jnp.full((1,), me, jnp.int32), a, swap(a, 1), b, swap(b, 1))
+    return placed, beside
 
 
 def spread(vector, width):
@@ -692,46 +932,52 @@
     groups = min(peers, 32)
     sub = peers // groups
 
-    small = jnp.concatenate(
-        [
-            spread(v.astype(bf16), width)
-            for v in (
-                attn_gain,
-                attn_bias,
-                query_bias,
-                value_bias,
-                output_bias,
-                mlp_gain,
-                mlp_bias,
-                reduce_bias,
-            )
-        ]
-    )
-    packed_one = jnp.concatenate([query_mat.astype(bf16), key_mat.astype(bf16), value_mat.astype(bf16), small])
-    first = gather(packed_one, [part] * 3 + [8], groups)
-
+    paired = peers == 32
     up = [(i, i + 1) for i in range(peers - 1)]
     down = [(i + 1, i) for i in range(peers - 1)]
+    own_ids = image_ids + 1
     normal_one, inv_one = norm_stats(tokens_in)
     normal_low = normal_one.astype(bf16)
-    before = lax.ppermute(normal_low[rows - RIM :], "dev", up)
-    after = lax.ppermute(normal_low[:RIM], "dev", down)
-    own_ids = image_ids + 1
-    ids_before = lax.ppermute(own_ids[rows - RIM :], "dev", up)
-    ids_after = lax.ppermute(own_ids[:RIM], "dev", down)
-    near_ids = jnp.concatenate([ids_before, own_ids, ids_after])
+
+    def with_ids(at):
+        ids = jnp.pad(own_ids[at], (0, width - RIM))
+        return jnp.concatenate(
+            [normal_low[at], (ids // 32).astype(bf16)[None], (ids % 32).astype(bf16)[None], jnp.zeros((6, width), bf16)]
+        )
+
+    before = lax.ppermute(with_ids(slice(rows - RIM, rows)), "dev", up)
+    after = lax.ppermute(with_ids(slice(0, RIM)), "dev", down)
+    smalls = (attn_gain, attn_bias, query_bias, value_bias, output_bias, mlp_gain, mlp_bias, reduce_bias)
+    if paired:
+        packed_one, packed_two = pack(
+            me, (query_mat, key_mat, value_mat), smalls, reduce_mat, expand_mat, output_mat, expand_bias
+        )
+        first, (before, after, packed_two) = doubling(packed_one, me, (before, after, packed_two))
+        second = gather(packed_two, (), groups)
+    else:
+        low = [v.astype(bf16) for v in (query_mat, key_mat, value_mat)]
+        packed_one = jnp.concatenate(low + [spread(v.astype(bf16), width) for v in smalls])
+        first = gather(packed_one, [part] * 3 + [8], groups)
+        expand_low = expand_mat.astype(bf16)
+        packed_two = jnp.concatenate(
+            [reduce_mat.astype(bf16)]
+            + [expand_low[:, i * width : (i + 1) * width] for i in range(fold)]
+            + [output_mat.astype(bf16), spread(expand_bias.astype(bf16), width), jnp.zeros((8 - fold, width), bf16)]
+        )
+        second = gather(packed_two, [fold * part] + [part] * (fold + 1) + [8], groups)
+
+
+    def ids_of(halo):
+        return (halo[RIM, :RIM].astype(f32) * 32 + halo[RIM + 1, :RIM].astype(f32)).astype(jnp.int32)
+
+    near_ids = jnp.concatenate([ids_of(before), own_ids, ids_of(after)])
+    before, after = before[:RIM], after[:RIM]
     ranges = key_ranges(own_ids, near_ids, rows // QB)
     key_ids, query_ids = near_ids[:, None], own_ids[None, :]
 
-    expand_low = expand_mat.astype(bf16)
-    second = jnp.concatenate(
-        [reduce_mat.astype(bf16)]
-        + [expand_low[:, i * width : (i + 1) * width] for i in range(fold)]
-        + [output_mat.astype(bf16), spread(expand_bias.astype(bf16), width), jnp.zeros((8 - fold, width), bf16)]
-    )
-    second, before, after = lax.optimization_barrier((second, before, after))
-    second = gather(second, [fold * part] + [part] * (fold + 1) + [8], groups)
-
+    first, before, after, ranges, key_ids, query_ids, normal_one = lax.optimization_barrier(
+        (first, before, after, ranges, key_ids, query_ids, normal_one)
+    )
     vectors = jnp.sum(first[:, groups * 0 + 3 * part * sub :].reshape(groups * sub, 8, width).astype(f32), axis=0)
     (gain_one, bias_one, bias_query, bias_value, bias_output, gain_two, bias_two, bias_reduce) = [
         vectors[i : i + 1] for i in range(8)
@@ -753,7 +999,7 @@
     normed_two = (normal_two * gain_two + bias_two).astype(bf16)
     branch_grad = out_grad.astype(bf16)
     block_out, normed_two_grad, expand_bias_grad, sums = mlp(
-        normed_two, branch_grad, middle, bias_reduce, bias_expand, second, (2 * fold + 1) * width // groups
+        normed_two, branch_grad, middle, bias_reduce, bias_expand, second, 2 * fold * width // groups + 8
     )
     reduce_bias_grad = column_sums(branch_grad)
     mlp_gain_grad = jnp.sum(normed_two_grad * normal_two, axis=0)
@@ -761,60 +1007,49 @@
     middle_grad = out_grad + norm_back(normed_two_grad, gain_two, normal_two, inv_two)
     attn_grad = middle_grad.astype(bf16)
     output_bias_grad = column_sums(attn_grad)
-    mixed_grad, sums = out_back(attn_grad, mixed, second, sums)
-    first_sum = scatter(sums, [fold * part] + [part] * (fold + 1))
-
+    first_sum = scatter(sums, [fold * part] + [part] * fold + [8 // sub])
+    place = jnp.full((1,), me if peers == 32 else 0, jnp.int32)
+    mixed_grad, *out_halves = out_back(attn_grad, mixed, second, 2 * fold, place)
+    out_other = swap(out_halves[1], 1) if peers == 32 else None
+    rest = jnp.concatenate(
+        [
+            output_bias_grad[None],
+            mlp_gain_grad[None],
+            mlp_bias_grad[None],
+            reduce_bias_grad[None],
+            expand_bias_grad.reshape(fold, width),
+            jnp.pad(head_top, (0, width - H))[None],
+        ]
+    )
+    mixed_grad, rest = lax.optimization_barrier((mixed_grad, rest))
     query_grad, key_near, value_near = attend_back(
         ranges, key_ids, query_ids, queries, near_kv, mixed_grad, mixed_wide, log_sums
     )
-    halves = qkv_grads(normed_near, query_grad, key_near, value_near, groups, me if peers == 32 else 0)
+    halves = qkv_grads(normed_near, query_grad, key_near, value_near, groups, place)
+    halves, query_grad, key_near, value_near = lax.optimization_barrier((halves, query_grad, key_near, value_near))
+    received = swap(halves[1], 1) if peers == 32 else None
+    normed_grad, to_prev, to_next, norm_sums = project_back(
+        query_grad, key_near, value_near, first, normal_one, before, after
+    )
+    from_next = lax.ppermute(to_prev, "dev", down)
+    from_prev = lax.ppermute(to_next, "dev", up)
+    totals = jnp.concatenate([norm_sums, rest])
     if peers == 32:
-        second_sum = halving(*halves)
+        second_sum, totals = halving((halves[0], received), (out_halves[0], out_other), totals)
     else:
-        order = [int(f"{i:05b}"[::-1], 2) for i in range(groups)]
-        joined = jnp.concatenate(halves, axis=0)
-        second_sum = scatter(jnp.stack([joined[i] for i in order]), [part] * 3)
-    outgoing = jnp.concatenate([key_near, value_near], axis=1)
-    from_next = lax.ppermute(outgoing[:RIM], "dev", down)
-    from_prev = lax.ppermute(outgoing[RIM + rows :], "dev", up)
-    own = outgoing[RIM : RIM + rows].astype(f32)
-    own = own + jnp.pad(from_prev.astype(f32), ((0, rows - RIM), (0, 0)))
-    own = own + jnp.pad(from_next.astype(f32), ((rows - RIM, 0), (0, 0)))
-    kv_grad = own.astype(bf16)
-    query_bias_grad = column_sums(query_grad)
-    value_bias_grad = column_sums(value_near)
-    normed_grad = project_back(query_grad, kv_grad, first)
-    attn_gain_grad = jnp.sum(normed_grad * normal_one, axis=0)
-    attn_bias_grad = jnp.sum(normed_grad, axis=0)
+        second_sum = plain((halves, out_halves), part)
+        bit = 1
+        while bit < peers:
+            totals = merge(totals, bit)
+            bit *= 2
+    normed_grad = normed_grad + jnp.pad(from_prev.astype(f32), ((0, rows - RIM), (0, 0)))
+    normed_grad = normed_grad + jnp.pad(from_next.astype(f32), ((rows - RIM, 0), (0, 0)))
     tokens_grad = middle_grad + norm_back(normed_grad, gain_one, normal_one, inv_one)
-
-    totals = jnp.stack(
-        [
-            attn_gain_grad,
-            attn_bias_grad,
-            query_bias_grad,
-            value_bias_grad,
-            output_bias_grad,
-            mlp_gain_grad,
-            mlp_bias_grad,
-            reduce_bias_grad,
-        ]
-    )
-    totals = jnp.concatenate(
-        [totals, expand_bias_grad.reshape(fold, width), jnp.pad(head_top, (0, width - H))[None]]
-    )
-    is_top = jnp.arange(totals.shape[0])[:, None] == totals.shape[0] - 1
-    bit = 1
-    while bit < peers:
-        other = lax.ppermute(totals, "dev", [(i, i ^ bit) for i in range(peers)])
-        totals = jnp.where(is_top, jnp.maximum(totals, other), totals + other)
-        bit *= 2
     mine = lax.dynamic_slice_in_dim(totals[:8], me * part, part, 1)
     expand_mine = lax.dynamic_slice_in_dim(totals[8 : 8 + fold].reshape(-1), me * part * fold, part * fold, 0)
     global_top = totals[-1, :H]
 
     first_sum = first_sum.astype(f32)
-    second_sum = second_sum.astype(f32)
     expand_out = jnp.concatenate(
         [first_sum[(fold + i) * part : (fold + i + 1) * part] for i in range(fold)], axis=1
     )
@@ -833,7 +1068,7 @@
         second_sum[part : 2 * part],
         second_sum[2 * part : 3 * part],
         mine[3],
-        first_sum[2 * fold * part :],
+        second_sum[3 * part :],
         mine[4],
         mine[5],
         mine[6],

time: 644 us -> 542 us (0.84)
  starting transfers between devices: 87.3 us -> 48.1 us
  Pallas kernels: 282 us -> 254 us
  other arithmetic: 66.3 us -> 46.4 us
  local copies, waits for them, and re-layouts: 37.4 us -> 25.7 us
  waiting for transfers between devices: 151 us -> 141 us
    ppermute x7 -> x21, waiting for transfers between devices: 40.8 us -> 130 us  [swap(): return lax.ppermute(value, 'dev', [(i, i ^ bit) for i in range(peers)])]
    all_gather x2 -> x1, waiting for transfers between devices: 95.9 us -> 11.3 us  [gather(): whole = lax.all_gather(value, 'dev', axis=0, tiled=True)]
    ppermute x11 -> x4, starting transfers between devices: 82 us -> 9.35 us  [the longest x1 4.08 us: local(): before = lax.ppermute(with_ids(slice(rows - RIM, rows)), 'dev', up)]
    ppermute x7 -> x21, starting transfers between devices: 5.18 us -> 38.7 us  [swap(): return lax.ppermute(value, 'dev', [(i, i ^ bit) for i in range(peers)])]
    pallas_call x1, Pallas kernels: 63 us -> 37.3 us  [attend(): pl.pallas_call(attend_kernel, grid_spec=pltpu.PrefetchScalarGridSpec(num_...]
    pallas_call x1, Pallas kernels: 77.2 us -> 53.1 us  [attend_back(): pl.pallas_call(attend_back_kernel, grid_spec=pltpu.PrefetchScalarGridSpec...]
    pallas_call x2 -> x4, Pallas kernels: 25.8 us -> 48.2 us  [the longest x1 28.3 us: project_back(): pl.pallas_call(normed_grad_kernel, grid=(3,), in_specs=[own, wide, wide,...]
    ppermute x11 -> x4, waiting for transfers between devices: 14.1 us -> 0.01 us  [the longest x1 0.01 us: local(): from_prev = lax.ppermute(to_next, 'dev', up)]
  transfers between devices with their start and end apart: 21 -> 27, of which waited for: 12 -> 13; matrix products, arithmetic and copies ran while one was open for 10% -> 9% of each run, Pallas kernels for 31% -> 34%
where the time goes in v2:
time: 542 us; the launch traced here: 535 us
  Pallas kernels  254 us (47%)
  waiting for transfers between devices  141 us (26%)
  starting transfers between devices  48.1 us (9%)
  other arithmetic  46.4 us (9%)
  local copies, waits for them, and re-layouts  25.7 us (5%)
  between operations  15.4 us (3%)
    ppermute x21, waiting for transfers between devices, swap(): return lax.ppermute(value, 'dev', [(i, i ^ bit) for i in range(peers)])  130 us
    pallas_call x1, Pallas kernels, mlp(): pl.pallas_call(mlp_kernel, grid=(fold,), in_specs=[pl.BlockSpec((rows, wi...  71.4 us
    pallas_call x1, Pallas kernels, attend_back(): pl.pallas_call(attend_back_kernel, grid_spec=pltpu.PrefetchScalarGridSpec...  53.1 us
    ppermute x21, starting transfers between devices, swap(): return lax.ppermute(value, 'dev', [(i, i ^ bit) for i in range(peers)])  38.7 us
    pallas_call x1, Pallas kernels, attend(): pl.pallas_call(attend_kernel, grid_spec=pltpu.PrefetchScalarGridSpec(num_...  37.3 us
    pallas_call x1, Pallas kernels, project_back(): pl.pallas_call(normed_grad_kernel, grid=(3,), in_specs=[own, wide, wide,...  28.3 us
    pallas_call x1, Pallas kernels, qkv_grads(): pl.pallas_call(qkv_grads_kernel, grid_spec=pltpu.PrefetchScalarGridSpec(n...  23.8 us
    pallas_call x1, Pallas kernels, project(): pl.pallas_call(qkv_kernel, grid=(3,), in_specs=[pl.BlockSpec((near, width...  20.5 us
  transfers between devices with their start and end apart: 27, of which 13 were waited for; matrix products, arithmetic and copies ran while one was open for 9% of the time, Pallas kernels for 34%

profile of v2, /device:TPU:0, one launch (start us, length us, event | category | flops | bytes accessed | tf_op | source)
XLA Modules:
  0.0 535.0 jit_solution(4325470991190403154)
XLA Ops:
  26.3 4.3 collective-permute-start
  30.6 17.4 %collective-permute-done = bf16[1,104,1024]{2,1,0:T(8,128)(2,1)S(1)} collective-permute-done((bf16[1,104,1024]{2,1,0:T(8,128)(2,1)}, bf16[1,104,1024]{2,1,0:T(8,128)(2,1)S(1)}, u32[]{:S(2)}, u32[]{:S(2)}) %collective-permute-start) | collective-permute-done | bytes 213024 | tf_op jit(solution)/shard_map/ppermute | solution.py:618
  49.0 8.1 %collective-permute-done.1 = bf16[2,104,1024]{2,1,0:T(8,128)(2,1)S(1)} collective-permute-done((bf16[2,104,1024]{2,1,0:T(8,128)(2,1)S(1)}, bf16[2,104,1024]{2,1,0:T(8,128)(2,1)S(1)}, u32[]{:S(2)}, u32[]{:S(2)}) %collective-permute-start.1) | collective-permute-done | bytes 426016 | tf_op jit(solution)/shard_map/ppermute | solution.py:618
  57.6 8.0 %collective-permute-done.7 = bf16[4,104,512]{2,1,0:T(8,128)(2,1)S(1)} collective-permute-done((bf16[4,104,512]{2,1,0:T(8,128)(2,1)S(1)}, bf16[4,104,512]{2,1,0:T(8,128)(2,1)S(1)}, u32[]{:S(2)}, u32[]{:S(2)}) %collective-permute-start.7) | collective-permute-done | bytes 426016 | tf_op jit(solution)/shard_map/ppermute | solution.py:618
  65.9 4.2 collective-permute-done.4
  70.4 21.4 %collective-permute-done.8 = bf16[8,104,512]{2,1,0:T(8,128)(2,1)S(1)} collective-permute-done((bf16[8,104,512]{2,1,0:T(8,128)(2,1)S(1)}, bf16[8,104,512]{2,1,0:T(8,128)(2,1)S(1)}, u32[]{:S(2)}, u32[]{:S(2)}) %collective-permute-start.8) | collective-permute-done | bytes 852000 | tf_op jit(solution)/shard_map/ppermute | solution.py:618
  103.7 6.2 %place.1.w_ref = bf16[32,104,1024]{2,1,0:T(8,128)(2,1)} custom-call(s32[1]{0:T(128)} %bitcast.me_ref, bf16[16,104,512]{2,1,0:T(8,128)(2,1)} %copy-done.11, bf16[16,104,512]{2,1,0:T(8,128)(2,1)} %collective-permute-done.6.ac_ref, bf16[16,104,512]{2,1,0:T(8,128)(2,1)} %copy-done.10, bf16[16,104,512]{2,1,0:T(8,128)(2,1)} %collective-permute-done.9.bc_ref), custom_call_target="tpu_custom_call" | custom-call | tf_op jit(solution)/shard_map/place/pallas_call | solution.py:883
  118.5 20.5 %qkv.1 = (bf16[1024,1024]{1,0:T(8,128)(2,1)}, bf16[2176,2048]{1,0:T(8,128)(2,1)}) custom-call(bf16[2176,1024]{1,0:T(8,128)(2,1)} %pad_maximum_fusion.a_ref, bf16[32,104,1024]{2,1,0:T(8,128)(2,1)} %place.1.w_ref, f32[1,3072]{1,0:T(1,128)} %pad_maximum_fusion.18.bias_ref), custom_call_target="tpu_custom_call" | custom-call | flops 11274289152 | bytes 22548578 | tf_op jit(solution)/shard_map/qkv/pallas_call | solution.py:521
  139.0 37.3 %attend.1 = (bf16[1024,1024]{1,0:T(8,128)(2,1)}, f32[1024,1024]{1,0:T(8,128)}, f32[4,1,4096]{2,1,0:T(1,128)}, f32[4,1,1024]{2,1,0:T(1,128)}) custom-call(s32[4]{0:T(128)} %get-tuple-element.79.low_ref, s32[4]{0:T(128)} %get-tuple-element.80.count_ref, s32[2176,1]{1,0:T(8,128)} %copy.58.key_ids_ref, s32[1,1024]{1,0:T(1,128)} %bitcast.149, ...), custom_call_target="tpu_custom_call" | custom-call | flops 14260633600 | bytes 28521268 | tf_op jit(solution)/shard_map/attend/pallas_call | solution.py:257
  176.2 11.3 %all-gather.2.cloned.1.call-done = bf16[9472,1024]{1,0:T(8,128)(2,1)} async-done(((bf16[296,1024]{1,0:T(8,128)(2,1)}), bf16[9472,1024]{1,0:T(8,128)(2,1)}) %all-gather.2.cloned.1.call-update) | async-done | bytes 19398672 | tf_op jit(solution)/shard_map/all_gather | solution.py:782
  198.1 71.4 %mlp.1 = (f32[1024,1024]{1,0:T(8,128)}, f32[1024,1024]{1,0:T(8,128)}, f32[1,4096]{1,0:T(1,128)}, bf16[32,264,1024]{2,1,0:T(8,128)(2,1)}) custom-call(bf16[1024,1024]{1,0:T(8,128)(2,1)} %add_convert_fusion.a_ref, bf16[1024,1024]{1,0:T(8,128)(2,1)} %get-tuple-element.136.dz_ref, f32[1024,1024]{1,0:T(8,128)} %copy-done, f32[1,1024]{1,0:T(1,128)} %get-tuple-element.176.rb_ref, ...), custom_call_target="tpu_custom_call" | custom-call | flops 51539607552 | bytes 103079216 | tf_op jit(solution)/shard_map/mlp/pallas_call | solution.py:387
  271.7 4.9 multiply_reduce_fusion.1
  278.4 5.5 %convert_reduce_fusion.1 = (f32[1024]{0:T(1024)S(1)}, bf16[1024,1024]{1,0:T(8,128)(2,1)}, f32[1024,1024]{1,0:T(8,128)}) fusion(f32[1024,1024]{1,0:T(8,128)S(1)} %copy-done.6, f32[1024]{0:T(1024)S(1)} %broadcast_multiply_fusion.4, f32[1024,1024]{1,0:T(8,128)S(1)} %copy-done.1, f32[1024]{0:T(1024)S(1)} %broadcast_multiply_fusion.6, ...), kind=kLoop, calls=%fused_computation.6 | loop fusion | flops 11533312 | bytes 18898944 | tf_op jit(solution)/shard_map/reduce_sum | solution.py:51
  284.0 11.3 %out_back.1 = (bf16[1024,1024]{1,0:T(8,128)(2,1)}, bf16[16,32,1024]{2,1,0:T(8,128)(2,1)}, bf16[16,32,1024]{2,1,0:T(8,128)(2,1)}) custom-call(s32[1]{0:T(128)} %bitcast.me_ref, bf16[1024,1024]{1,0:T(8,128)(2,1)} %get-tuple-element.138.ag_ref, bf16[1024,1024]{1,0:T(8,128)(2,1)} %get-tuple-element.89.mixed_ref, bf16[32,296,1024]{2,1,0:T(8,128)(2,1)} %bitcast.126), custom_call_target="tpu_custom_call" | custom-call | flops 4294967296 | bytes 8589934 | tf_op jit(solution)/shard_map/out_back/pallas_call | solution.py:463
  295.3 53.1 %attend_back.1 = (bf16[1024,1024]{1,0:T(8,128)(2,1)}, bf16[2176,1024]{1,0:T(8,128)(2,1)}, bf16[2176,1024]{1,0:T(8,128)(2,1)}) custom-call(s32[4]{0:T(128)} %get-tuple-element.79.low_ref, s32[4]{0:T(128)} %get-tuple-element.80.count_ref, s32[2176,1]{1,0:T(8,128)} %copy.58.key_ids_ref, s32[1,1024]{1,0:T(1,128)} %bitcast.150, ...), custom_call_target="tpu_custom_call" | custom-call | flops 28521267200 | bytes 57042536 | tf_op jit(solution)/shard_map/attend_back/pallas_call | solution.py:283
  348.4 23.8 %qkv_grads.1 = (bf16[16,96,1024]{2,1,0:T(8,128)(2,1)}, bf16[16,96,1024]{2,1,0:T(8,128)(2,1)}) custom-call(s32[1]{0:T(128)} %bitcast.me_ref, bf16[2176,1024]{1,0:T(8,128)(2,1)} %pad_maximum_fusion.a_ref, bf16[1024,1024]{1,0:T(8,128)(2,1)} %get-tuple-element.104.dq_ref, bf16[2176,1024]{1,0:T(8,128)(2,1)} %get-tuple-element.105.dk_ref, ...), custom_call_target="tpu_custom_call" | custom-call | flops 11274289152 | bytes 22548578 | tf_op jit(solution)/shard_map/qkv_grads/pallas_call | solution.py:592
  372.2 6.3 %collective-permute-start.12 = (bf16[16,96,1024]{2,1,0:T(8,128)(2,1)}, bf16[16,96,1024]{2,1,0:T(8,128)(2,1)S(1)}, u32[]{:S(2)}, u32[]{:S(2)}) collective-permute-start(bf16[16,96,1024]{2,1,0:T(8,128)(2,1)} %get-tuple-element.111), channel_id=1, source_target_pairs={{0,1},{1,0},{2,3},{3,2},{4,5},{5,4},{6,7},{7,6},{8,9},{9,8},{10,11... | collective-permute-start | bytes 9437192 | tf_op jit(solution)/shard_map/ppermute | solution.py:618
  378.5 28.3 %normed_grad.1 = (f32[1024,1024]{1,0:T(8,128)}, bf16[576,1024]{1,0:T(8,128)(2,1)}, bf16[576,1024]{1,0:T(8,128)(2,1)}, f32[4,1024]{1,0:T(4,128)}) custom-call(bf16[1024,1024]{1,0:T(8,128)(2,1)} %get-tuple-element.104.dq_ref, bf16[2176,1024]{1,0:T(8,128)(2,1)} %get-tuple-element.105.dk_ref, bf16[2176,1024]{1,0:T(8,128)(2,1)} %get-tuple-element.106.dv_ref, ...), custom_call_target="tpu_custom_call" | custom-call | flops 11274289152 | bytes 22548578 | tf_op jit(solution)/shard_map/normed_grad/pallas_call | solution.py:756
  419.0 6.0 %collective-permute-start.14 = (bf16[2,4,64,1024]{3,2,1,0:T(8,128)(2,1)S(1)}, bf16[2,4,64,1024]{3,2,1,0:T(8,128)(2,1)S(1)}, u32[]{:S(2)}, u32[]{:S(2)}) collective-permute-start(bf16[2,4,64,1024]{3,2,1,0:T(8,128)(2,1)S(1)} %add_convert_fusion.4), channel_id=1, source_target_pairs={{0,2},{1,3},{2,0},{3,1},{4,6},{5,7},{6,4},{7,5},{8,10},{9,11},{10,... | collective-permute-start | bytes 3145736 | tf_op jit(solution)/shard_map/ppermute | solution.py:618
  428.5 36.2 %collective-permute-done.15 = bf16[2,4,64,1024]{3,2,1,0:T(8,128)(2,1)S(1)} collective-permute-done((bf16[2,4,64,1024]{3,2,1,0:T(8,128)(2,1)S(1)}, bf16[2,4,64,1024]{3,2,1,0:T(8,128)(2,1)S(1)}, u32[]{:S(2)}, u32[]{:S(2)}) %collective-permute-start.15) | collective-permute-done | bytes 1048608 | tf_op jit(solution)/shard_map/ppermute | solution.py:618
  465.6 6.9 %collective-permute-start.19 = (f32[13,1024]{1,0:T(8,128)S(1)}, f32[13,1024]{1,0:T(8,128)S(1)}, u32[]{:S(2)}, u32[]{:S(2)}) collective-permute-start(f32[13,1024]{1,0:T(8,128)S(1)} %pad_maximum_fusion.14), channel_id=1, source_target_pairs={{0,2},{1,3},{2,0},{3,1},{4,6},{5,7},{6,4},{7,5},{8,10},{9,11},{10,... | collective-permute-start | bytes 159752 | tf_op jit(solution)/shard_map/ppermute | solution.py:618
  477.4 10.0 %collective-permute-done.17 = bf16[4,64,1024]{2,1,0:T(8,128)(2,1)S(1)} collective-permute-done((bf16[4,64,1024]{2,1,0:T(8,128)(2,1)S(1)}, bf16[4,64,1024]{2,1,0:T(8,128)(2,1)S(1)}, u32[]{:S(2)}, u32[]{:S(2)}) %collective-permute-start.17) | collective-permute-done | bytes 524320 | tf_op jit(solution)/shard_map/ppermute | solution.py:618
  493.5 8.1 %collective-permute-done.20 = bf16[2,128,1024]{2,1,0:T(8,128)(2,1)S(1)} collective-permute-done((bf16[2,128,1024]{2,1,0:T(8,128)(2,1)S(1)}, bf16[2,128,1024]{2,1,0:T(8,128)(2,1)S(1)}, u32[]{:S(2)}, u32[]{:S(2)}) %collective-permute-start.20) | collective-permute-done | bytes 524320 | tf_op jit(solution)/shard_map/ppermute | solution.py:618
  515.2 8.8 %collective-permute-done.24 = bf16[128,1024]{1,0:T(8,128)(2,1)S(1)} collective-permute-done((bf16[128,1024]{1,0:T(8,128)(2,1)S(1)}, bf16[128,1024]{1,0:T(8,128)(2,1)S(1)}, u32[]{:S(2)}, u32[]{:S(2)}) %collective-permute-start.24) | collective-permute-done | bytes 262176 | tf_op jit(solution)/shard_map/ppermute | solution.py:618
  (247 shorter events, 100.1 us)
Async XLA Ops:
  7.2 180.3 %all-gather.2.cloned.1.call-start = ((), (), s32[]{:S(2)}) async-start(), calls=%async_computation.1 | async-start | bytes 20004864 | tf_op jit(solution)/shard_map/all_gather | solution.py:782
  16.6 40.6 %collective-permute-start.3 = (bf16[584,1024]{1,0:T(8,128)(2,1)S(1)}, bf16[584,1024]{1,0:T(8,128)(2,1)}, u32[]{:S(2)}, u32[]{:S(2)}) collective-permute-start(bf16[584,1024]{1,0:T(8,128)(2,1)S(1)} %get-tuple-element.201), channel_id=1, source_target_pairs={{1,0},{2,1},{3,2},{4,3},{5,4},{6,5},{7,6},{8,7},{9,8},{10,9},{11,1... | collective-permute-start | bytes 3588104 | tf_op jit(solution)/shard_map/ppermute | solution.py:949
  17.9 39.3 %collective-permute-start.2 = (bf16[584,1024]{1,0:T(8,128)(2,1)S(1)}, bf16[584,1024]{1,0:T(8,128)(2,1)}, u32[]{:S(2)}, u32[]{:S(2)}) collective-permute-start(bf16[584,1024]{1,0:T(8,128)(2,1)S(1)} %get-tuple-element.202), channel_id=1, source_target_pairs={{0,1},{1,2},{2,3},{3,4},{4,5},{5,6},{6,7},{7,8},{8,9},{9,10},{10,1... | collective-permute-start | bytes 3588104 | tf_op jit(solution)/shard_map/ppermute | solution.py:948
  26.3 21.7 %collective-permute-start = (bf16[1,104,1024]{2,1,0:T(8,128)(2,1)}, bf16[1,104,1024]{2,1,0:T(8,128)(2,1)S(1)}, u32[]{:S(2)}, u32[]{:S(2)}) collective-permute-start(bf16[1,104,1024]{2,1,0:T(8,128)(2,1)} %bitcast.137), channel_id=1, source_target_pairs={{0,16},{1,17},{2,18},{3,19},{4,20},{5,21},{6,22},{7,23},{8,24},{9,... | collective-permute-start | bytes 638984 | tf_op jit(solution)/shard_map/ppermute | solution.py:618
  49.0 8.2 %collective-permute-start.1 = (bf16[2,104,1024]{2,1,0:T(8,128)(2,1)S(1)}, bf16[2,104,1024]{2,1,0:T(8,128)(2,1)S(1)}, u32[]{:S(2)}, u32[]{:S(2)}) collective-permute-start(bf16[2,104,1024]{2,1,0:T(8,128)(2,1)S(1)} %pad_maximum_fusion.9), channel_id=1, source_target_pairs={{0,8},{1,9},{2,10},{3,11},{4,12},{5,13},{6,14},{7,15},{8,0},{9,1},... | collective-permute-start | bytes 1277960 | tf_op jit(solution)/shard_map/ppermute | solution.py:618
  57.2 467.8 %reduce-scatter.2.cloned.1.call-start = ((), (), s32[]{:S(2)}) async-start(), calls=%async_computation.2 | async-start | bytes 17842176 | tf_op jit(solution)/shard_map/reduce_scatter | solution.py:806
  57.4 8.2 %collective-permute-start.7 = (bf16[4,104,512]{2,1,0:T(8,128)(2,1)S(1)}, bf16[4,104,512]{2,1,0:T(8,128)(2,1)S(1)}, u32[]{:S(2)}, u32[]{:S(2)}) collective-permute-start(bf16[4,104,512]{2,1,0:T(8,128)(2,1)S(1)} %pad_maximum_fusion.11), channel_id=1, source_target_pairs={{0,4},{1,5},{2,6},{3,7},{4,0},{5,1},{6,2},{7,3},{8,12},{9,13},{10,... | collective-permute-start | bytes 1277960 | tf_op jit(solution)/shard_map/ppermute | solution.py:618
  57.5 12.6 %collective-permute-start.4 = (bf16[4,104,512]{2,1,0:T(8,128)(2,1)S(1)}, bf16[4,104,512]{2,1,0:T(8,128)(2,1)S(1)}, u32[]{:S(2)}, u32[]{:S(2)}) collective-permute-start(bf16[4,104,512]{2,1,0:T(8,128)(2,1)S(1)} %pad_maximum_fusion.10), channel_id=1, source_target_pairs={{0,2},{1,3},{2,0},{3,1},{4,6},{5,7},{6,4},{7,5},{8,10},{9,11},{10,... | collective-permute-start | bytes 1277960 | tf_op jit(solution)/shard_map/ppermute | solution.py:618
  65.6 26.1 %collective-permute-start.8 = (bf16[8,104,512]{2,1,0:T(8,128)(2,1)S(1)}, bf16[8,104,512]{2,1,0:T(8,128)(2,1)S(1)}, u32[]{:S(2)}, u32[]{:S(2)}) collective-permute-start(bf16[8,104,512]{2,1,0:T(8,128)(2,1)S(1)} %pad_maximum_fusion.5), channel_id=1, source_target_pairs={{0,2},{1,3},{2,0},{3,1},{4,6},{5,7},{6,4},{7,5},{8,10},{9,11},{10,... | collective-permute-start | bytes 2555912 | tf_op jit(solution)/shard_map/ppermute | solution.py:618
  70.2 21.9 %collective-permute-start.5 = (bf16[8,104,512]{2,1,0:T(8,128)(2,1)S(1)}, bf16[8,104,512]{2,1,0:T(8,128)(2,1)S(1)}, u32[]{:S(2)}, u32[]{:S(2)}) collective-permute-start(bf16[8,104,512]{2,1,0:T(8,128)(2,1)S(1)} %pad_maximum_fusion.4), channel_id=1, source_target_pairs={{0,4},{1,5},{2,6},{3,7},{4,0},{5,1},{6,2},{7,3},{8,12},{9,13},{10,... | collective-permute-start | bytes 2555912 | tf_op jit(solution)/shard_map/ppermute | solution.py:618
  92.0 11.7 %collective-permute-start.9 = (bf16[16,104,512]{2,1,0:T(8,128)(2,1)S(1)}, bf16[16,104,512]{2,1,0:T(8,128)(2,1)}, u32[]{:S(2)}, u32[]{:S(2)}) collective-permute-start(bf16[16,104,512]{2,1,0:T(8,128)(2,1)S(1)} %pad_maximum_fusion.2.b_ref), channel_id=1, source_target_pairs={{0,1},{1,0},{2,3},{3,2},{4,5},{5,4},{6,7},{7,6},{8,9},{9,8},{10,11... | collective-permute-start | bytes 5111816 | tf_op jit(solution)/shard_map/ppermute | solution.py:618
  92.2 11.4 %collective-permute-start.6 = (bf16[16,104,512]{2,1,0:T(8,128)(2,1)S(1)}, bf16[16,104,512]{2,1,0:T(8,128)(2,1)}, u32[]{:S(2)}, u32[]{:S(2)}) collective-permute-start(bf16[16,104,512]{2,1,0:T(8,128)(2,1)S(1)} %pad_maximum_fusion.1.a_ref), channel_id=1, source_target_pairs={{0,1},{1,0},{2,3},{3,2},{4,5},{5,4},{6,7},{7,6},{8,9},{9,8},{10,11... | collective-permute-start | bytes 5111816 | tf_op jit(solution)/shard_map/ppermute | solution.py:618
  372.2 43.9 %collective-permute-start.12 = (bf16[16,96,1024]{2,1,0:T(8,128)(2,1)}, bf16[16,96,1024]{2,1,0:T(8,128)(2,1)S(1)}, u32[]{:S(2)}, u32[]{:S(2)}) collective-permute-start(bf16[16,96,1024]{2,1,0:T(8,128)(2,1)} %get-tuple-element.111), channel_id=1, source_target_pairs={{0,1},{1,0},{2,3},{3,2},{4,5},{5,4},{6,7},{7,6},{8,9},{9,8},{10,11... | collective-permute-start | bytes 9437192 | tf_op jit(solution)/shard_map/ppermute | solution.py:618
  378.5 36.3 %collective-permute-start.13 = (bf16[16,32,1024]{2,1,0:T(8,128)(2,1)}, bf16[16,32,1024]{2,1,0:T(8,128)(2,1)S(1)}, u32[]{:S(2)}, u32[]{:S(2)}) collective-permute-start(bf16[16,32,1024]{2,1,0:T(8,128)(2,1)} %get-tuple-element.113), channel_id=1, source_target_pairs={{0,1},{1,0},{2,3},{3,2},{4,5},{5,4},{6,7},{7,6},{8,9},{9,8},{10,11... | collective-permute-start | bytes 3145736 | tf_op jit(solution)/shard_map/ppermute | solution.py:618
  406.8 65.7 %collective-permute-start.10 = (bf16[576,1024]{1,0:T(8,128)(2,1)}, bf16[576,1024]{1,0:T(8,128)(2,1)S(1)}, u32[]{:S(2)}, u32[]{:S(2)}) collective-permute-start(bf16[576,1024]{1,0:T(8,128)(2,1)} %get-tuple-element.108), channel_id=1, source_target_pairs={{0,1},{1,2},{2,3},{3,4},{4,5},{5,6},{6,7},{7,8},{8,9},{9,10},{10,1... | collective-permute-start | bytes 3538952 | tf_op jit(solution)/shard_map/ppermute | solution.py:1035
  409.5 63.0 %collective-permute-start.11 = (bf16[576,1024]{1,0:T(8,128)(2,1)}, bf16[576,1024]{1,0:T(8,128)(2,1)S(1)}, u32[]{:S(2)}, u32[]{:S(2)}) collective-permute-start(bf16[576,1024]{1,0:T(8,128)(2,1)} %get-tuple-element.109), channel_id=1, source_target_pairs={{1,0},{2,1},{3,2},{4,3},{5,4},{6,5},{7,6},{8,7},{9,8},{10,9},{11,1... | collective-permute-start | bytes 3538952 | tf_op jit(solution)/shard_map/ppermute | solution.py:1034
  417.8 10.7 %collective-permute-start.16 = (f32[13,1024]{1,0:T(8,128)S(1)}, f32[13,1024]{1,0:T(8,128)S(1)}, u32[]{:S(2)}, u32[]{:S(2)}) collective-permute-start(f32[13,1024]{1,0:T(8,128)S(1)} %pad_maximum_fusion.13), channel_id=1, source_target_pairs={{0,1},{1,0},{2,3},{3,2},{4,5},{5,4},{6,7},{7,6},{8,9},{9,8},{10,11... | collective-permute-start | bytes 159752 | tf_op jit(solution)/shard_map/ppermute | solution.py:618
  419.0 46.2 %collective-permute-start.14 = (bf16[2,4,64,1024]{3,2,1,0:T(8,128)(2,1)S(1)}, bf16[2,4,64,1024]{3,2,1,0:T(8,128)(2,1)S(1)}, u32[]{:S(2)}, u32[]{:S(2)}) collective-permute-start(bf16[2,4,64,1024]{3,2,1,0:T(8,128)(2,1)S(1)} %add_convert_fusion.4), channel_id=1, source_target_pairs={{0,2},{1,3},{2,0},{3,1},{4,6},{5,7},{6,4},{7,5},{8,10},{9,11},{10,... | collective-permute-start | bytes 3145736 | tf_op jit(solution)/shard_map/ppermute | solution.py:618
  425.0 39.7 %collective-permute-start.15 = (bf16[2,4,64,1024]{3,2,1,0:T(8,128)(2,1)S(1)}, bf16[2,4,64,1024]{3,2,1,0:T(8,128)(2,1)S(1)}, u32[]{:S(2)}, u32[]{:S(2)}) collective-permute-start(bf16[2,4,64,1024]{3,2,1,0:T(8,128)(2,1)S(1)} %pad_maximum_fusion.3), channel_id=1, source_target_pairs={{0,4},{1,5},{2,6},{3,7},{4,0},{5,1},{6,2},{7,3},{8,12},{9,13},{10,... | collective-permute-start | bytes 3145736 | tf_op jit(solution)/shard_map/ppermute | solution.py:618
  465.6 11.8 %collective-permute-start.19 = (f32[13,1024]{1,0:T(8,128)S(1)}, f32[13,1024]{1,0:T(8,128)S(1)}, u32[]{:S(2)}, u32[]{:S(2)}) collective-permute-start(f32[13,1024]{1,0:T(8,128)S(1)} %pad_maximum_fusion.14), channel_id=1, source_target_pairs={{0,2},{1,3},{2,0},{3,1},{4,6},{5,7},{6,4},{7,5},{8,10},{9,11},{10,... | collective-permute-start | bytes 159752 | tf_op jit(solution)/shard_map/ppermute | solution.py:618
  473.6 13.9 %collective-permute-start.17 = (bf16[4,64,1024]{2,1,0:T(8,128)(2,1)S(1)}, bf16[4,64,1024]{2,1,0:T(8,128)(2,1)S(1)}, u32[]{:S(2)}, u32[]{:S(2)}) collective-permute-start(bf16[4,64,1024]{2,1,0:T(8,128)(2,1)S(1)} %get-tuple-element.119), channel_id=1, source_target_pairs={{0,4},{1,5},{2,6},{3,7},{4,0},{5,1},{6,2},{7,3},{8,12},{9,13},{10,... | collective-permute-start | bytes 1572872 | tf_op jit(solution)/shard_map/ppermute | solution.py:618
  476.1 12.8 %collective-permute-start.18 = (bf16[4,64,1024]{2,1,0:T(8,128)(2,1)S(1)}, bf16[4,64,1024]{2,1,0:T(8,128)(2,1)S(1)}, u32[]{:S(2)}, u32[]{:S(2)}) collective-permute-start(bf16[4,64,1024]{2,1,0:T(8,128)(2,1)S(1)} %get-tuple-element.120), channel_id=1, source_target_pairs={{0,2},{1,3},{2,0},{3,1},{4,6},{5,7},{6,4},{7,5},{8,10},{9,11},{10,... | collective-permute-start | bytes 1572872 | tf_op jit(solution)/shard_map/ppermute | solution.py:618
  489.7 12.0 %collective-permute-start.20 = (bf16[2,128,1024]{2,1,0:T(8,128)(2,1)S(1)}, bf16[2,128,1024]{2,1,0:T(8,128)(2,1)S(1)}, u32[]{:S(2)}, u32[]{:S(2)}) collective-permute-start(bf16[2,128,1024]{2,1,0:T(8,128)(2,1)S(1)} %pad_maximum_fusion.7), channel_id=1, source_target_pairs={{0,8},{1,9},{2,10},{3,11},{4,12},{5,13},{6,14},{7,15},{8,0},{9,1},... | collective-permute-start | bytes 1572872 | tf_op jit(solution)/shard_map/ppermute | solution.py:618
  513.0 11.0 %collective-permute-start.24 = (bf16[128,1024]{1,0:T(8,128)(2,1)S(1)}, bf16[128,1024]{1,0:T(8,128)(2,1)S(1)}, u32[]{:S(2)}, u32[]{:S(2)}) collective-permute-start(bf16[128,1024]{1,0:T(8,128)(2,1)S(1)} %fusion.9), channel_id=1, source_target_pairs={{0,16},{1,17},{2,18},{3,19},{4,20},{5,21},{6,22},{7,23},{8,24},{9,... | collective-permute-start | bytes 786440 | tf_op jit(solution)/shard_map/ppermute | solution.py:618
  (40 other events, 347.0 us)
Sparse Core Ops, SparseCore 0:
  57.3 130.1 all-gather.1
  269.7 214.6 reduce-scatter.1
